TPU v7x, 512 devices: a whole 4x8x8 slice. The times are simulated.
512 devices in a mesh: row: 32 (over z, x), col: 16 (over y, core).
Axes of the slice: x: 4, y: 8, z: 8, core: 2. Of those that a mesh axis runs over, the one named last changes fastest.
Arguments:
- rhs: bfloat16 [524288, 256], P(('row', 'col')), may hold values from -6 to 6
- order: int32 [512, 1024], P(('row', 'col')), may hold values from 0 to 1023, each once within a row
- leaf_inverse: bfloat16 [1024, 512, 512], P(('row', 'col')), may hold values from -1 to 2
- leaf_column_generator: bfloat16 [1024, 512, 256], P(('row', 'col')), may hold values from -0.25 to 0.25
- factor_up: bfloat16 [512, 9, 256, 256], P(('row', 'col')), may hold values from -1 to 1
- downward_coupling_factors: bfloat16 [512, 9, 256, 256], P(('row', 'col')), may hold values from -1 to 2
Outputs:
- solution: bfloat16 [524288, 256], P(('row', 'col'))
All inputs are finite; a program needn't handle non-finite values.
Results may differ from a plain program's by a relative error of at most 0.015.
Values may be sent and summed in bfloat16 or wider, within the bound.
No kernel may reach another device: no remote copies, remote signals or barrier semaphores. Data moves between devices by JAX's collectives and lax.ppermute only.
A program may use at most 64 MiB of HBM per device.

v0:
```python
import jax
import jax.numpy as jnp
from jax import lax
from jax.sharding import PartitionSpec as P


def from_partner(x, axis, bit):
    return lax.ppermute(x, axis, [(i, i ^ 1 << bit) for i in range(lax.axis_size(axis))])


def up_partner(value, level, col_bits):
    if level < col_bits:
        return from_partner(value, "col", level)
    return from_partner(value, "row", level - col_bits)


def down_partner(value, level, col_bits):
    if level < col_bits:
        return from_partner(value, "col", level)
    return from_partner(value, "row", level - col_bits)


def times(kernel_matrix, value):
    return jnp.dot(kernel_matrix, value, preferred_element_type=jnp.float32)


def times_transposed(kernel_matrix, value):
    return jnp.einsum("ji,jg->ig", kernel_matrix, value, preferred_element_type=jnp.float32)


def on_device(
    rhs, order, leaf_inverse, leaf_column_generator, factor_up, downward_coupling_factors
):
    positions = order[0]
    leaves = leaf_inverse.shape[0]
    leaf = leaf_inverse.shape[1]
    genes = rhs.shape[1]
    ordered = jnp.take(rhs, positions, axis=0)
    blocks = ordered.reshape(leaves, leaf, genes)
    eliminated_rows = jnp.einsum(
        "jab,jbg->jag", leaf_inverse, blocks, preferred_element_type=jnp.float32
    )
    elimination_portion = eliminated_rows.astype(jnp.bfloat16)
    solve_state = jnp.einsum(
        "dmq,dms->qs",
        leaf_column_generator,
        elimination_portion,
        preferred_element_type=jnp.float32,
    )
    up_mats = factor_up[0]
    down_mats = downward_coupling_factors[0]
    levels = up_mats.shape[0]
    col_bits = lax.axis_size("col").bit_length() - 1
    saved = []
    for level in range(levels):
        saved.append(solve_state)
        term = times(up_mats[level], solve_state.astype(jnp.bfloat16)).astype(jnp.bfloat16)
        partner_values = up_partner(term, level, col_bits)
        solve_state = term.astype(jnp.float32) + partner_values.astype(jnp.float32)
    top = solve_state
    for level in reversed(range(levels)):
        rounded = top.astype(jnp.bfloat16)
        own = times_transposed(up_mats[level], rounded)
        sent = times(down_mats[level], rounded).astype(jnp.bfloat16)
        partner_values = down_partner(sent, level, col_bits)
        top = saved[level] + 0.5 * (partner_values.astype(jnp.float32) - own)
    top_half = top.astype(jnp.bfloat16)
    back = jnp.einsum(
        "jar,rg->jag", leaf_column_generator, top_half, preferred_element_type=jnp.float32
    ).astype(jnp.bfloat16)
    solved = eliminated_rows - jnp.einsum(
        "jab,jbg->jag", leaf_inverse, back, preferred_element_type=jnp.float32
    )
    flat = solved.reshape(leaves * leaf, genes).astype(jnp.bfloat16)
    placed = jnp.zeros((leaves * leaf, genes), jnp.bfloat16)
    return placed.at[positions].set(flat)


def solution(mesh):
    in_specs = (
        P(("row", "col"), None),
        P(("row", "col"), None),
        P(("row", "col"), None, None),
        P(("row", "col"), None, None),
        P(("row", "col"), None, None, None),
        P(("row", "col"), None, None, None),
    )
    out_specs = P(("row", "col"), None)
    return jax.shard_map(
        on_device, mesh=mesh, in_specs=in_specs, out_specs=out_specs, check_vma=False
    )
```

profile of v0, /device:TPU:1, one launch (start us, length us, event | category | flops | bytes accessed | tf_op | source)
XLA Modules:
  0.0 183.1 jit_solution(12997550748986146038)
XLA Ops:
  2.7 4.6 %gather_fusion = bf16[1024,256]{1,0:T(8,128)(2,1)S(1)} fusion(bf16[1024,256]{1,0:T(8,128)(2,1)} %param.6, s32[1024]{0:T(1024)S(1)} %broadcast_clamp_fusion), kind=kCustom, calls=%fused_computation | custom fusion | bytes 1052672 | tf_op jit(solution)/shard_map/jit(_take)/gather | solution.py:38
  10.0 8.7 %collective-permute-start = (bf16[256,256]{0,1:T(8,128)(2,1)S(1)}, bf16[256,256]{0,1:T(8,128)(2,1)S(1)}, u32[]{:S(2)}, u32[]{:S(2)}) collective-permute-start(bf16[256,256]{0,1:T(8,128)(2,1)S(1)} %fusion.3), channel_id=1, source_target_pairs={{0,1},{1,0},{2,3},{3,2},{4,5},{5,4},{6,7},{7,6},{8,9},{9,8},{10,11... | collective-permute-start | bytes 393224 | tf_op jit(solution)/shard_map/ppermute | solution.py:8
  21.9 4.7 %collective-permute-done.1 = bf16[256,256]{0,1:T(8,128)(2,1)S(1)} collective-permute-done((bf16[256,256]{0,1:T(8,128)(2,1)S(1)}, bf16[256,256]{0,1:T(8,128)(2,1)S(1)}, u32[]{:S(2)}, u32[]{:S(2)}) %collective-permute-start.1) | collective-permute-done | bytes 131104 | tf_op jit(solution)/shard_map/ppermute | solution.py:8
  28.7 9.1 %collective-permute-done.2 = bf16[256,256]{0,1:T(8,128)(2,1)S(1)} collective-permute-done((bf16[256,256]{0,1:T(8,128)(2,1)S(1)}, bf16[256,256]{0,1:T(8,128)(2,1)S(1)}, u32[]{:S(2)}, u32[]{:S(2)}) %collective-permute-start.2) | collective-permute-done | bytes 131104 | tf_op jit(solution)/shard_map/ppermute | solution.py:8
  40.0 8.4 %collective-permute-done.3 = bf16[256,256]{0,1:T(8,128)(2,1)S(1)} collective-permute-done((bf16[256,256]{0,1:T(8,128)(2,1)S(1)}, bf16[256,256]{0,1:T(8,128)(2,1)S(1)}, u32[]{:S(2)}, u32[]{:S(2)}) %collective-permute-start.3) | collective-permute-done | bytes 131104 | tf_op jit(solution)/shard_map/ppermute | solution.py:8
  50.7 3.8 %collective-permute-done.4 = bf16[256,256]{0,1:T(8,128)(2,1)S(1)} collective-permute-done((bf16[256,256]{0,1:T(8,128)(2,1)S(1)}, bf16[256,256]{0,1:T(8,128)(2,1)S(1)}, u32[]{:S(2)}, u32[]{:S(2)}) %collective-permute-start.4) | collective-permute-done | bytes 131104 | tf_op jit(solution)/shard_map/ppermute | solution.py:8
  56.6 5.3 %collective-permute-done.5 = bf16[256,256]{0,1:T(8,128)(2,1)S(1)} collective-permute-done((bf16[256,256]{0,1:T(8,128)(2,1)S(1)}, bf16[256,256]{0,1:T(8,128)(2,1)S(1)}, u32[]{:S(2)}, u32[]{:S(2)}) %collective-permute-start.5) | collective-permute-done | bytes 131104 | tf_op jit(solution)/shard_map/ppermute | solution.py:8
  64.1 3.8 %collective-permute-done.6 = bf16[256,256]{0,1:T(8,128)(2,1)S(1)} collective-permute-done((bf16[256,256]{0,1:T(8,128)(2,1)S(1)}, bf16[256,256]{0,1:T(8,128)(2,1)S(1)}, u32[]{:S(2)}, u32[]{:S(2)}) %collective-permute-start.6) | collective-permute-done | bytes 131104 | tf_op jit(solution)/shard_map/ppermute | solution.py:8
  70.0 6.0 %collective-permute-done.7 = bf16[256,256]{0,1:T(8,128)(2,1)S(1)} collective-permute-done((bf16[256,256]{0,1:T(8,128)(2,1)S(1)}, bf16[256,256]{0,1:T(8,128)(2,1)S(1)}, u32[]{:S(2)}, u32[]{:S(2)}) %collective-permute-start.7) | collective-permute-done | bytes 131104 | tf_op jit(solution)/shard_map/ppermute | solution.py:8
  76.2 5.6 %collective-permute-start.8 = (bf16[256,256]{0,1:T(8,128)(2,1)S(1)}, bf16[256,256]{0,1:T(8,128)(2,1)S(1)}, u32[]{:S(2)}, u32[]{:S(2)}) collective-permute-start(bf16[256,256]{0,1:T(8,128)(2,1)S(1)} %fusion.11), channel_id=1, source_target_pairs={{0,256},{16,272},{32,288},{48,304},{64,320},{80,336},{96,352},{112... | collective-permute-start | bytes 393224 | tf_op jit(solution)/shard_map/ppermute | solution.py:8
  81.8 4.2 %collective-permute-done.8 = bf16[256,256]{0,1:T(8,128)(2,1)S(1)} collective-permute-done((bf16[256,256]{0,1:T(8,128)(2,1)S(1)}, bf16[256,256]{0,1:T(8,128)(2,1)S(1)}, u32[]{:S(2)}, u32[]{:S(2)}) %collective-permute-start.8) | collective-permute-done | bytes 131104 | tf_op jit(solution)/shard_map/ppermute | solution.py:8
  86.2 6.7 %collective-permute-start.9 = (bf16[256,256]{0,1:T(8,128)(2,1)S(1)}, bf16[256,256]{0,1:T(8,128)(2,1)S(1)}, u32[]{:S(2)}, u32[]{:S(2)}) collective-permute-start(bf16[256,256]{0,1:T(8,128)(2,1)S(1)} %fusion.12), channel_id=1, source_target_pairs={{0,256},{16,272},{32,288},{48,304},{64,320},{80,336},{96,352},{112... | collective-permute-start | bytes 393224 | tf_op jit(solution)/shard_map/ppermute | solution.py:8
  92.9 3.4 %collective-permute-done.9 = bf16[256,256]{0,1:T(8,128)(2,1)S(1)} collective-permute-done((bf16[256,256]{0,1:T(8,128)(2,1)S(1)}, bf16[256,256]{0,1:T(8,128)(2,1)S(1)}, u32[]{:S(2)}, u32[]{:S(2)}) %collective-permute-start.9) | collective-permute-done | bytes 131104 | tf_op jit(solution)/shard_map/ppermute | solution.py:8
  96.7 6.3 %collective-permute-start.10 = (bf16[256,256]{0,1:T(8,128)(2,1)S(1)}, bf16[256,256]{0,1:T(8,128)(2,1)S(1)}, u32[]{:S(2)}, u32[]{:S(2)}) collective-permute-start(bf16[256,256]{0,1:T(8,128)(2,1)S(1)} %fusion.13), channel_id=1, source_target_pairs={{0,128},{16,144},{32,160},{48,176},{64,192},{80,208},{96,224},{112... | collective-permute-start | bytes 393224 | tf_op jit(solution)/shard_map/ppermute | solution.py:8
  105.8 4.0 %collective-permute-start.11 = (bf16[256,256]{0,1:T(8,128)(2,1)S(1)}, bf16[256,256]{0,1:T(8,128)(2,1)S(1)}, u32[]{:S(2)}, u32[]{:S(2)}) collective-permute-start(bf16[256,256]{0,1:T(8,128)(2,1)S(1)} %fusion.14), channel_id=1, source_target_pairs={{0,64},{16,80},{32,96},{48,112},{64,0},{80,16},{96,32},{112,48},{1... | collective-permute-start | bytes 393224 | tf_op jit(solution)/shard_map/ppermute | solution.py:8
  109.9 3.7 %collective-permute-done.11 = bf16[256,256]{0,1:T(8,128)(2,1)S(1)} collective-permute-done((bf16[256,256]{0,1:T(8,128)(2,1)S(1)}, bf16[256,256]{0,1:T(8,128)(2,1)S(1)}, u32[]{:S(2)}, u32[]{:S(2)}) %collective-permute-start.11) | collective-permute-done | bytes 131104 | tf_op jit(solution)/shard_map/ppermute | solution.py:8
  117.3 3.9 %collective-permute-done.12 = bf16[256,256]{0,1:T(8,128)(2,1)S(1)} collective-permute-done((bf16[256,256]{0,1:T(8,128)(2,1)S(1)}, bf16[256,256]{0,1:T(8,128)(2,1)S(1)}, u32[]{:S(2)}, u32[]{:S(2)}) %collective-permute-start.12) | collective-permute-done | bytes 131104 | tf_op jit(solution)/shard_map/ppermute | solution.py:8
  123.7 3.6 %collective-permute-done.13 = bf16[256,256]{0,1:T(8,128)(2,1)S(1)} collective-permute-done((bf16[256,256]{0,1:T(8,128)(2,1)S(1)}, bf16[256,256]{0,1:T(8,128)(2,1)S(1)}, u32[]{:S(2)}, u32[]{:S(2)}) %collective-permute-start.13) | collective-permute-done | bytes 131104 | tf_op jit(solution)/shard_map/ppermute | solution.py:8
  127.8 6.8 %collective-permute-start.14 = (bf16[256,256]{0,1:T(8,128)(2,1)S(1)}, bf16[256,256]{0,1:T(8,128)(2,1)S(1)}, u32[]{:S(2)}, u32[]{:S(2)}) collective-permute-start(bf16[256,256]{0,1:T(8,128)(2,1)S(1)} %fusion.17), channel_id=1, source_target_pairs={{0,8},{1,9},{2,10},{3,11},{4,12},{5,13},{6,14},{7,15},{8,0},{9,1},... | collective-permute-start | bytes 393224 | tf_op jit(solution)/shard_map/ppermute | solution.py:8
  139.8 4.7 %collective-permute-done.15 = bf16[256,256]{0,1:T(8,128)(2,1)S(1)} collective-permute-done((bf16[256,256]{0,1:T(8,128)(2,1)S(1)}, bf16[256,256]{0,1:T(8,128)(2,1)S(1)}, u32[]{:S(2)}, u32[]{:S(2)}) %collective-permute-start.15) | collective-permute-done | bytes 131104 | tf_op jit(solution)/shard_map/ppermute | solution.py:8
  144.9 3.7 %collective-permute-start.16 = (bf16[256,256]{0,1:T(8,128)(2,1)S(1)}, bf16[256,256]{0,1:T(8,128)(2,1)S(1)}, u32[]{:S(2)}, u32[]{:S(2)}) collective-permute-start(bf16[256,256]{0,1:T(8,128)(2,1)S(1)} %fusion.19), channel_id=1, source_target_pairs={{0,2},{1,3},{2,0},{3,1},{4,6},{5,7},{6,4},{7,5},{8,10},{9,11},{10,... | collective-permute-start | bytes 393224 | tf_op jit(solution)/shard_map/ppermute | solution.py:8
  148.6 3.7 %collective-permute-done.16 = bf16[256,256]{0,1:T(8,128)(2,1)S(1)} collective-permute-done((bf16[256,256]{0,1:T(8,128)(2,1)S(1)}, bf16[256,256]{0,1:T(8,128)(2,1)S(1)}, u32[]{:S(2)}, u32[]{:S(2)}) %collective-permute-start.16) | collective-permute-done | bytes 131104 | tf_op jit(solution)/shard_map/ppermute | solution.py:8
  152.8 21.0 %collective-permute-start.17 = (bf16[256,256]{0,1:T(8,128)(2,1)S(1)}, bf16[256,256]{0,1:T(8,128)(2,1)S(1)}, u32[]{:S(2)}, u32[]{:S(2)}) collective-permute-start(bf16[256,256]{0,1:T(8,128)(2,1)S(1)} %fusion.20), channel_id=1, source_target_pairs={{0,1},{1,0},{2,3},{3,2},{4,5},{5,4},{6,7},{7,6},{8,9},{9,8},{10,11... | collective-permute-start | bytes 393224 | tf_op jit(solution)/shard_map/ppermute | solution.py:8
  177.4 5.7 %scatter_custom_fusion = bf16[1024,256]{1,0:T(8,128)(2,1)} fusion(s32[1024]{0:T(1024)S(1)} %bitcast.206, bf16[1024,256]{1,0:T(8,128)(2,1)S(1)} %bitcast.204, bf16[]{:T(256)} %constant.6.clone.1), kind=kCustom, calls=%fused_computation.77 | custom fusion | bytes 524290 | tf_op jit(solution)/shard_map/scatter | solution.py:76
  (60 shorter events, 41.3 us)
Async XLA Ops:
  0.0 7.5 %copy-start = (bf16[2,512,512]{2,1,0:T(8,128)(2,1)S(1)}, bf16[2,512,512]{2,1,0:T(8,128)(2,1)}, u32[]{:S(2)}) copy-start(bf16[2,512,512]{2,1,0:T(8,128)(2,1)} %param.8) | copy-start | bytes 3145732
  7.5 1.0 copy-start.2
  8.5 1.3 copy-start.1
  10.0 9.7 %collective-permute-start = (bf16[256,256]{0,1:T(8,128)(2,1)S(1)}, bf16[256,256]{0,1:T(8,128)(2,1)S(1)}, u32[]{:S(2)}, u32[]{:S(2)}) collective-permute-start(bf16[256,256]{0,1:T(8,128)(2,1)S(1)} %fusion.3), channel_id=1, source_target_pairs={{0,1},{1,0},{2,3},{3,2},{4,5},{5,4},{6,7},{7,6},{8,9},{9,8},{10,11... | collective-permute-start | bytes 393224 | tf_op jit(solution)/shard_map/ppermute | solution.py:8
  20.0 6.6 %collective-permute-start.1 = (bf16[256,256]{0,1:T(8,128)(2,1)S(1)}, bf16[256,256]{0,1:T(8,128)(2,1)S(1)}, u32[]{:S(2)}, u32[]{:S(2)}) collective-permute-start(bf16[256,256]{0,1:T(8,128)(2,1)S(1)} %fusion.4), channel_id=1, source_target_pairs={{0,2},{1,3},{2,0},{3,1},{4,6},{5,7},{6,4},{7,5},{8,10},{9,11},{10,... | collective-permute-start | bytes 393224 | tf_op jit(solution)/shard_map/ppermute | solution.py:8
  26.8 11.0 %collective-permute-start.2 = (bf16[256,256]{0,1:T(8,128)(2,1)S(1)}, bf16[256,256]{0,1:T(8,128)(2,1)S(1)}, u32[]{:S(2)}, u32[]{:S(2)}) collective-permute-start(bf16[256,256]{0,1:T(8,128)(2,1)S(1)} %fusion.5), channel_id=1, source_target_pairs={{0,4},{1,5},{2,6},{3,7},{4,0},{5,1},{6,2},{7,3},{8,12},{9,13},{10,... | collective-permute-start | bytes 393224 | tf_op jit(solution)/shard_map/ppermute | solution.py:8
  38.0 10.3 %collective-permute-start.3 = (bf16[256,256]{0,1:T(8,128)(2,1)S(1)}, bf16[256,256]{0,1:T(8,128)(2,1)S(1)}, u32[]{:S(2)}, u32[]{:S(2)}) collective-permute-start(bf16[256,256]{0,1:T(8,128)(2,1)S(1)} %fusion.6), channel_id=1, source_target_pairs={{0,8},{1,9},{2,10},{3,11},{4,12},{5,13},{6,14},{7,15},{8,0},{9,1},... | collective-permute-start | bytes 393224 | tf_op jit(solution)/shard_map/ppermute | solution.py:8
  48.6 37.4 %copy-start.3 = (bf16[1,9,256,256]{3,2,1,0:T(8,128)(2,1)S(1)}, bf16[1,9,256,256]{3,2,1,0:T(8,128)(2,1)}, u32[]{:S(2)}) copy-start(bf16[1,9,256,256]{3,2,1,0:T(8,128)(2,1)} %param.11) | copy-start | bytes 3538948
  48.6 5.8 %collective-permute-start.4 = (bf16[256,256]{0,1:T(8,128)(2,1)S(1)}, bf16[256,256]{0,1:T(8,128)(2,1)S(1)}, u32[]{:S(2)}, u32[]{:S(2)}) collective-permute-start(bf16[256,256]{0,1:T(8,128)(2,1)S(1)} %fusion.7), channel_id=1, source_target_pairs={{0,16},{16,0},{32,48},{48,32},{64,80},{80,64},{96,112},{112,96},{1... | collective-permute-start | bytes 393224 | tf_op jit(solution)/shard_map/ppermute | solution.py:8
  54.7 7.2 %collective-permute-start.5 = (bf16[256,256]{0,1:T(8,128)(2,1)S(1)}, bf16[256,256]{0,1:T(8,128)(2,1)S(1)}, u32[]{:S(2)}, u32[]{:S(2)}) collective-permute-start(bf16[256,256]{0,1:T(8,128)(2,1)S(1)} %fusion.8), channel_id=1, source_target_pairs={{0,32},{16,48},{32,0},{48,16},{64,96},{80,112},{96,64},{112,80},{1... | collective-permute-start | bytes 393224 | tf_op jit(solution)/shard_map/ppermute | solution.py:8
  62.1 5.7 %collective-permute-start.6 = (bf16[256,256]{0,1:T(8,128)(2,1)S(1)}, bf16[256,256]{0,1:T(8,128)(2,1)S(1)}, u32[]{:S(2)}, u32[]{:S(2)}) collective-permute-start(bf16[256,256]{0,1:T(8,128)(2,1)S(1)} %fusion.9), channel_id=1, source_target_pairs={{0,64},{16,80},{32,96},{48,112},{64,0},{80,16},{96,32},{112,48},{1... | collective-permute-start | bytes 393224 | tf_op jit(solution)/shard_map/ppermute | solution.py:8
  68.1 7.9 %collective-permute-start.7 = (bf16[256,256]{0,1:T(8,128)(2,1)S(1)}, bf16[256,256]{0,1:T(8,128)(2,1)S(1)}, u32[]{:S(2)}, u32[]{:S(2)}) collective-permute-start(bf16[256,256]{0,1:T(8,128)(2,1)S(1)} %fusion.10), channel_id=1, source_target_pairs={{0,128},{16,144},{32,160},{48,176},{64,192},{80,208},{96,224},{112... | collective-permute-start | bytes 393224 | tf_op jit(solution)/shard_map/ppermute | solution.py:8
  76.2 9.8 %collective-permute-start.8 = (bf16[256,256]{0,1:T(8,128)(2,1)S(1)}, bf16[256,256]{0,1:T(8,128)(2,1)S(1)}, u32[]{:S(2)}, u32[]{:S(2)}) collective-permute-start(bf16[256,256]{0,1:T(8,128)(2,1)S(1)} %fusion.11), channel_id=1, source_target_pairs={{0,256},{16,272},{32,288},{48,304},{64,320},{80,336},{96,352},{112... | collective-permute-start | bytes 393224 | tf_op jit(solution)/shard_map/ppermute | solution.py:8
  86.2 10.1 %collective-permute-start.9 = (bf16[256,256]{0,1:T(8,128)(2,1)S(1)}, bf16[256,256]{0,1:T(8,128)(2,1)S(1)}, u32[]{:S(2)}, u32[]{:S(2)}) collective-permute-start(bf16[256,256]{0,1:T(8,128)(2,1)S(1)} %fusion.12), channel_id=1, source_target_pairs={{0,256},{16,272},{32,288},{48,304},{64,320},{80,336},{96,352},{112... | collective-permute-start | bytes 393224 | tf_op jit(solution)/shard_map/ppermute | solution.py:8
  96.7 8.6 %collective-permute-start.10 = (bf16[256,256]{0,1:T(8,128)(2,1)S(1)}, bf16[256,256]{0,1:T(8,128)(2,1)S(1)}, u32[]{:S(2)}, u32[]{:S(2)}) collective-permute-start(bf16[256,256]{0,1:T(8,128)(2,1)S(1)} %fusion.13), channel_id=1, source_target_pairs={{0,128},{16,144},{32,160},{48,176},{64,192},{80,208},{96,224},{112... | collective-permute-start | bytes 393224 | tf_op jit(solution)/shard_map/ppermute | solution.py:8
  105.8 7.7 %collective-permute-start.11 = (bf16[256,256]{0,1:T(8,128)(2,1)S(1)}, bf16[256,256]{0,1:T(8,128)(2,1)S(1)}, u32[]{:S(2)}, u32[]{:S(2)}) collective-permute-start(bf16[256,256]{0,1:T(8,128)(2,1)S(1)} %fusion.14), channel_id=1, source_target_pairs={{0,64},{16,80},{32,96},{48,112},{64,0},{80,16},{96,32},{112,48},{1... | collective-permute-start | bytes 393224 | tf_op jit(solution)/shard_map/ppermute | solution.py:8
  114.0 7.2 %collective-permute-start.12 = (bf16[256,256]{0,1:T(8,128)(2,1)S(1)}, bf16[256,256]{0,1:T(8,128)(2,1)S(1)}, u32[]{:S(2)}, u32[]{:S(2)}) collective-permute-start(bf16[256,256]{0,1:T(8,128)(2,1)S(1)} %fusion.15), channel_id=1, source_target_pairs={{0,32},{16,48},{32,0},{48,16},{64,96},{80,112},{96,64},{112,80},{1... | collective-permute-start | bytes 393224 | tf_op jit(solution)/shard_map/ppermute | solution.py:8
  121.6 5.7 %collective-permute-start.13 = (bf16[256,256]{0,1:T(8,128)(2,1)S(1)}, bf16[256,256]{0,1:T(8,128)(2,1)S(1)}, u32[]{:S(2)}, u32[]{:S(2)}) collective-permute-start(bf16[256,256]{0,1:T(8,128)(2,1)S(1)} %fusion.16), channel_id=1, source_target_pairs={{0,16},{16,0},{32,48},{48,32},{64,80},{80,64},{96,112},{112,96},{1... | collective-permute-start | bytes 393224 | tf_op jit(solution)/shard_map/ppermute | solution.py:8
  127.8 9.6 %collective-permute-start.14 = (bf16[256,256]{0,1:T(8,128)(2,1)S(1)}, bf16[256,256]{0,1:T(8,128)(2,1)S(1)}, u32[]{:S(2)}, u32[]{:S(2)}) collective-permute-start(bf16[256,256]{0,1:T(8,128)(2,1)S(1)} %fusion.17), channel_id=1, source_target_pairs={{0,8},{1,9},{2,10},{3,11},{4,12},{5,13},{6,14},{7,15},{8,0},{9,1},... | collective-permute-start | bytes 393224 | tf_op jit(solution)/shard_map/ppermute | solution.py:8
  137.8 6.6 %collective-permute-start.15 = (bf16[256,256]{0,1:T(8,128)(2,1)S(1)}, bf16[256,256]{0,1:T(8,128)(2,1)S(1)}, u32[]{:S(2)}, u32[]{:S(2)}) collective-permute-start(bf16[256,256]{0,1:T(8,128)(2,1)S(1)} %fusion.18), channel_id=1, source_target_pairs={{0,4},{1,5},{2,6},{3,7},{4,0},{5,1},{6,2},{7,3},{8,12},{9,13},{10,... | collective-permute-start | bytes 393224 | tf_op jit(solution)/shard_map/ppermute | solution.py:8
  144.9 7.5 %collective-permute-start.16 = (bf16[256,256]{0,1:T(8,128)(2,1)S(1)}, bf16[256,256]{0,1:T(8,128)(2,1)S(1)}, u32[]{:S(2)}, u32[]{:S(2)}) collective-permute-start(bf16[256,256]{0,1:T(8,128)(2,1)S(1)} %fusion.19), channel_id=1, source_target_pairs={{0,2},{1,3},{2,0},{3,1},{4,6},{5,7},{6,4},{7,5},{8,10},{9,11},{10,... | collective-permute-start | bytes 393224 | tf_op jit(solution)/shard_map/ppermute | solution.py:8
  152.8 22.0 %collective-permute-start.17 = (bf16[256,256]{0,1:T(8,128)(2,1)S(1)}, bf16[256,256]{0,1:T(8,128)(2,1)S(1)}, u32[]{:S(2)}, u32[]{:S(2)}) collective-permute-start(bf16[256,256]{0,1:T(8,128)(2,1)S(1)} %fusion.20), channel_id=1, source_target_pairs={{0,1},{1,0},{2,3},{3,2},{4,5},{5,4},{6,7},{7,6},{8,9},{9,8},{10,11... | collective-permute-start | bytes 393224 | tf_op jit(solution)/shard_map/ppermute | solution.py:8
where the time goes:
time: 184 us; the launch traced here: 183 us
  starting transfers between devices  83.7 us (45%)
  waiting for transfers between devices  75.1 us (41%)
  local copies, waits for them, and re-layouts  13.8 us (8%)
  matrix products  7.91 us (4%)
  other arithmetic  2.14 us (1%)
    ppermute x18, starting transfers between devices, from_partner(): lax.ppermute(x, axis, [(i, i ^ 1 << bit) for i in range(lax.axis_size(axi...  83.7 us
    ppermute x18, waiting for transfers between devices, from_partner(): lax.ppermute(x, axis, [(i, i ^ 1 << bit) for i in range(lax.axis_size(axi...  75.1 us
    scatter x1, local copies, waits for them, and re-layouts, on_device(): return placed.at[positions].set(flat)  5.72 us
    gather x2, local copies, waits for them, and re-layouts, on_device(): ordered = jnp.take(rhs, positions, axis=0)  4.78 us
    dot_general x18, matrix products, times(): return jnp.dot(kernel_matrix, value, preferred_element_type=jnp.float32)  3.96 us
  transfers between devices with their start and end apart: 18, of which 18 were waited for; matrix products, arithmetic and copies ran while one was open for 0% of the time, Pallas kernels for 0%

commit v1 on v0

--- a/solution.py
+++ b/solution.py
@@ -4,20 +4,25 @@
 from jax.sharding import PartitionSpec as P
 
 
-def from_partner(x, axis, bit):
-    return lax.ppermute(x, axis, [(i, i ^ 1 << bit) for i in range(lax.axis_size(axis))])
+def pair_groups(size, bit):
+    step = 1 << bit
+    return [[i, i ^ step] for i in range(size) if not i & step]
 
 
-def up_partner(value, level, col_bits):
-    if level < col_bits:
-        return from_partner(value, "col", level)
-    return from_partner(value, "row", level - col_bits)
+def axis_of(level, col_bits):
+    return ("col", level) if level < col_bits else ("row", level - col_bits)
 
 
-def down_partner(value, level, col_bits):
-    if level < col_bits:
-        return from_partner(value, "col", level)
-    return from_partner(value, "row", level - col_bits)
+def both(value, level, col_bits):
+    axis, bit = axis_of(level, col_bits)
+    groups = pair_groups(lax.axis_size(axis), bit)
+    return lax.all_gather(value, axis, axis=0, tiled=False, axis_index_groups=groups)
+
+
+def partner_part(pair, level, col_bits):
+    axis, bit = axis_of(level, col_bits)
+    high = (lax.axis_index(axis) >> bit) & 1
+    return jnp.where(high == 1, pair[0], pair[1])
 
 
 def times(kernel_matrix, value):
@@ -50,20 +55,28 @@
     up_mats = factor_up[0]
     down_mats = downward_coupling_factors[0]
     levels = up_mats.shape[0]
+    last = levels - 1
     col_bits = lax.axis_size("col").bit_length() - 1
     saved = []
     for level in range(levels):
         saved.append(solve_state)
         term = times(up_mats[level], solve_state.astype(jnp.bfloat16)).astype(jnp.bfloat16)
-        partner_values = up_partner(term, level, col_bits)
-        solve_state = term.astype(jnp.float32) + partner_values.astype(jnp.float32)
+        if level == last:
+            pair = both(jnp.stack([term, down_mats[level]]), level, col_bits)
+            terms, coupling = pair[:, 0], pair[:, 1]
+        else:
+            terms = both(term, level, col_bits)
+        solve_state = terms[0].astype(jnp.float32) + terms[1].astype(jnp.float32)
     top = solve_state
     for level in reversed(range(levels)):
         rounded = top.astype(jnp.bfloat16)
         own = times_transposed(up_mats[level], rounded)
-        sent = times(down_mats[level], rounded).astype(jnp.bfloat16)
-        partner_values = down_partner(sent, level, col_bits)
-        top = saved[level] + 0.5 * (partner_values.astype(jnp.float32) - own)
+        if level == last:
+            coupled = times(partner_part(coupling, level, col_bits), rounded).astype(jnp.bfloat16)
+        else:
+            sent = times(down_mats[level], rounded).astype(jnp.bfloat16)
+            coupled = partner_part(both(sent, level, col_bits), level, col_bits)
+        top = saved[level] + 0.5 * (coupled.astype(jnp.float32) - own)
     top_half = top.astype(jnp.bfloat16)
     back = jnp.einsum(
         "jar,rg->jag", leaf_column_generator, top_half, preferred_element_type=jnp.float32

time: 184 us -> 177 us (0.962)
  blocking collectives: 0 us -> 134 us
  starting transfers between devices: 83.7 us -> 0 us
  waiting for transfers between devices: 75.1 us -> 0 us
  matrix products: 7.91 us -> 23.9 us
  local copies, waits for them, and re-layouts: 13.8 us -> 16.5 us
    all_gather x0 -> x17, blocking collectives: none -> 134 us  [both(): lax.all_gather(value, axis, axis=0, tiled=False, axis_index_groups=groups)]
    ppermute x18 -> x0, starting transfers between devices: 83.7 us -> none  [from_partner(): lax.ppermute(x, axis, [(i, i ^ 1 << bit) for i in range(lax.axis_size(axi...]
    ppermute x18 -> x0, waiting for transfers between devices: 75.1 us -> none  [from_partner(): lax.ppermute(x, axis, [(i, i ^ 1 << bit) for i in range(lax.axis_size(axi...]
    dot_general x9, matrix products: 1.77 us -> 11.1 us  [times_transposed(): jnp.einsum('ji,jg->ig', kernel_matrix, value, preferred_element_type=jnp....]
    dot_general x18, matrix products: 3.96 us -> 11.5 us  [times(): return jnp.dot(kernel_matrix, value, preferred_element_type=jnp.float32)]
    unnamed x9 -> x54, local copies, waits for them, and re-layouts: 2.05 us -> 5.69 us
  transfers between devices with their start and end apart: 18 -> 0, of which waited for: 18 -> 0; matrix products, arithmetic and copies ran while one was open for 0% -> 0% of each run, Pallas kernels for 0% -> 0%
where the time goes in v1:
time: 177 us; the launch traced here: 176 us
  blocking collectives  134 us (76%)
  matrix products  23.9 us (14%)
  local copies, waits for them, and re-layouts  16.5 us (9%)
    all_gather x17, blocking collectives, both(): lax.all_gather(value, axis, axis=0, tiled=False, axis_index_groups=groups)  134 us
    dot_general x18, matrix products, times(): return jnp.dot(kernel_matrix, value, preferred_element_type=jnp.float32)  11.5 us
    dot_general x9, matrix products, times_transposed(): jnp.einsum('ji,jg->ig', kernel_matrix, value, preferred_element_type=jnp....  11.1 us
    scatter x1, local copies, waits for them, and re-layouts, on_device(): return placed.at[positions].set(flat)  5.72 us
    unnamed x54, local copies, waits for them, and re-layouts  5.69 us
    gather x2, local copies, waits for them, and re-layouts, on_device(): ordered = jnp.take(rhs, positions, axis=0)  4.79 us

profile of v1, /device:TPU:1, one launch (start us, length us, event | category | flops | bytes accessed | tf_op | source)
XLA Modules:
  0.0 176.1 jit_solution(16829505348105095303)
XLA Ops:
  0.8 4.6 %gather_fusion = bf16[1024,256]{1,0:T(8,128)(2,1)S(1)} fusion(bf16[1024,256]{1,0:T(8,128)(2,1)} %param.6, s32[1024]{0:T(1024)S(1)} %broadcast_clamp_fusion), kind=kCustom, calls=%fused_computation | custom fusion | bytes 1052672 | tf_op jit(solution)/shard_map/jit(_take)/gather | solution.py:43
  9.4 8.5 %all-gather = bf16[512,256]{0,1:T(8,128)(2,1)S(1)} all-gather(bf16[256,256]{0,1:T(8,128)(2,1)S(1)} %fusion.41), channel_id=2, replica_groups={{0,1},{2,3},{4,5},{6,7},{8,9},{10,11},{12,13},{14,15},{16,17},{18,19},{..., dimensions={0}, use_global_device_ids=true | all-gather | bytes 393216 | tf_op jit(solution)/shard_map/all_gather | solution.py:19
  18.1 5.3 %all-gather.1 = bf16[512,256]{0,1:T(8,128)(2,1)S(1)} all-gather(bf16[256,256]{0,1:T(8,128)(2,1)S(1)} %fusion.42), channel_id=3, replica_groups={{0,2},{1,3},{4,6},{5,7},{8,10},{9,11},{12,14},{13,15},{16,18},{17,19},{..., dimensions={0}, use_global_device_ids=true | all-gather | bytes 393216 | tf_op jit(solution)/shard_map/all_gather | solution.py:19
  23.6 9.8 %all-gather.2 = bf16[512,256]{0,1:T(8,128)(2,1)S(1)} all-gather(bf16[256,256]{0,1:T(8,128)(2,1)S(1)} %fusion.43), channel_id=4, replica_groups={{0,4},{1,5},{2,6},{3,7},{8,12},{9,13},{10,14},{11,15},{16,20},{17,21},{..., dimensions={0}, use_global_device_ids=true | all-gather | bytes 393216 | tf_op jit(solution)/shard_map/all_gather | solution.py:19
  33.7 9.0 %all-gather.3 = bf16[512,256]{0,1:T(8,128)(2,1)S(1)} all-gather(bf16[256,256]{0,1:T(8,128)(2,1)S(1)} %fusion.44), channel_id=5, replica_groups={{0,8},{1,9},{2,10},{3,11},{4,12},{5,13},{6,14},{7,15},{16,24},{17,25},{..., dimensions={0}, use_global_device_ids=true | all-gather | bytes 393216 | tf_op jit(solution)/shard_map/all_gather | solution.py:19
  42.9 4.5 %all-gather.4 = bf16[512,256]{0,1:T(8,128)(2,1)S(1)} all-gather(bf16[256,256]{0,1:T(8,128)(2,1)S(1)} %fusion.45), channel_id=6, replica_groups={{0,16},{32,48},{64,80},{96,112},{128,144},{160,176},{192,208},{224,240}..., dimensions={0}, use_global_device_ids=true | all-gather | bytes 393216 | tf_op jit(solution)/shard_map/all_gather | solution.py:19
  47.6 6.0 %all-gather.5 = bf16[512,256]{0,1:T(8,128)(2,1)S(1)} all-gather(bf16[256,256]{0,1:T(8,128)(2,1)S(1)} %fusion.46), channel_id=7, replica_groups={{0,32},{16,48},{64,96},{80,112},{128,160},{144,176},{192,224},{208,240}..., dimensions={0}, use_global_device_ids=true | all-gather | bytes 393216 | tf_op jit(solution)/shard_map/all_gather | solution.py:19
  53.9 4.5 %all-gather.6 = bf16[512,256]{0,1:T(8,128)(2,1)S(1)} all-gather(bf16[256,256]{0,1:T(8,128)(2,1)S(1)} %fusion.47), channel_id=8, replica_groups={{0,64},{16,80},{32,96},{48,112},{128,192},{144,208},{160,224},{176,240}..., dimensions={0}, use_global_device_ids=true | all-gather | bytes 393216 | tf_op jit(solution)/shard_map/all_gather | solution.py:19
  58.6 6.5 %all-gather.7 = bf16[512,256]{0,1:T(8,128)(2,1)S(1)} all-gather(bf16[256,256]{0,1:T(8,128)(2,1)S(1)} %fusion.48), channel_id=9, replica_groups={{0,128},{16,144},{32,160},{48,176},{64,192},{80,208},{96,224},{112,240}..., dimensions={0}, use_global_device_ids=true | all-gather | bytes 393216 | tf_op jit(solution)/shard_map/all_gather | solution.py:19
  66.1 12.7 %all-gather.8 = bf16[4,256,256]{2,1,0:T(8,128)(2,1)} all-gather(bf16[2,256,256]{2,1,0:T(8,128)(2,1)S(1)} %copy.16), channel_id=10, replica_groups={{0,256},{16,272},{32,288},{48,304},{64,320},{80,336},{96,352},{112,368}..., dimensions={0}, use_global_device_ids=true | all-gather | bytes 786432 | tf_op jit(solution)/shard_map/all_gather | solution.py:19
  78.8 1.4 fusion.39
  82.2 11.8 %all-gather.9 = bf16[512,256]{0,1:T(8,128)(2,1)} all-gather(bf16[256,256]{0,1:T(8,128)(2,1)S(1)} %fusion.50), channel_id=11, replica_groups={{0,128},{16,144},{32,160},{48,176},{64,192},{80,208},{96,224},{112,240}..., dimensions={0}, use_global_device_ids=true | all-gather | bytes 393216 | tf_op jit(solution)/shard_map/all_gather | solution.py:19
  94.0 1.3 fusion.31
  96.5 4.7 %all-gather.10 = bf16[512,256]{0,1:T(8,128)(2,1)} all-gather(bf16[256,256]{0,1:T(8,128)(2,1)S(1)} %fusion.51), channel_id=12, replica_groups={{0,64},{16,80},{32,96},{48,112},{128,192},{144,208},{160,224},{176,240}..., dimensions={0}, use_global_device_ids=true | all-gather | bytes 393216 | tf_op jit(solution)/shard_map/all_gather | solution.py:19
  104.2 6.2 %all-gather.11 = bf16[512,256]{0,1:T(8,128)(2,1)} all-gather(bf16[256,256]{0,1:T(8,128)(2,1)S(1)} %fusion.52), channel_id=13, replica_groups={{0,32},{16,48},{64,96},{80,112},{128,160},{144,176},{192,224},{208,240}..., dimensions={0}, use_global_device_ids=true | all-gather | bytes 393216 | tf_op jit(solution)/shard_map/all_gather | solution.py:19
  110.4 1.3 fusion.33
  113.5 4.8 %all-gather.12 = bf16[512,256]{0,1:T(8,128)(2,1)} all-gather(bf16[256,256]{0,1:T(8,128)(2,1)S(1)} %fusion.53), channel_id=14, replica_groups={{0,16},{32,48},{64,80},{96,112},{128,144},{160,176},{192,208},{224,240}..., dimensions={0}, use_global_device_ids=true | all-gather | bytes 393216 | tf_op jit(solution)/shard_map/all_gather | solution.py:19
  118.3 1.3 fusion.34
  120.7 8.6 %all-gather.13 = bf16[512,256]{0,1:T(8,128)(2,1)} all-gather(bf16[256,256]{0,1:T(8,128)(2,1)S(1)} %fusion.54), channel_id=15, replica_groups={{0,8},{1,9},{2,10},{3,11},{4,12},{5,13},{6,14},{7,15},{16,24},{17,25},{..., dimensions={0}, use_global_device_ids=true | all-gather | bytes 393216 | tf_op jit(solution)/shard_map/all_gather | solution.py:19
  132.4 5.7 %all-gather.14 = bf16[512,256]{0,1:T(8,128)(2,1)} all-gather(bf16[256,256]{0,1:T(8,128)(2,1)S(1)} %fusion.55), channel_id=16, replica_groups={{0,4},{1,5},{2,6},{3,7},{8,12},{9,13},{10,14},{11,15},{16,20},{17,21},{..., dimensions={0}, use_global_device_ids=true | all-gather | bytes 393216 | tf_op jit(solution)/shard_map/all_gather | solution.py:19
  138.1 1.3 fusion.36
  141.2 7.5 %all-gather.15 = bf16[512,256]{0,1:T(8,128)(2,1)S(1)} all-gather(bf16[256,256]{0,1:T(8,128)(2,1)S(1)} %fusion.56), channel_id=17, replica_groups={{0,2},{1,3},{4,6},{5,7},{8,10},{9,11},{12,14},{13,15},{16,18},{17,19},{..., dimensions={0}, use_global_device_ids=true | all-gather | bytes 393216 | tf_op jit(solution)/shard_map/all_gather | solution.py:19
  150.9 17.6 %all-gather.16 = bf16[512,256]{0,1:T(8,128)(2,1)S(1)} all-gather(bf16[256,256]{0,1:T(8,128)(2,1)S(1)} %fusion.57), channel_id=18, replica_groups={{0,1},{2,3},{4,5},{6,7},{8,9},{10,11},{12,13},{14,15},{16,17},{18,19},{..., dimensions={0}, use_global_device_ids=true | all-gather | bytes 393216 | tf_op jit(solution)/shard_map/all_gather | solution.py:19
  170.4 5.7 %scatter_custom_fusion = bf16[1024,256]{1,0:T(8,128)(2,1)} fusion(s32[1024]{0:T(1024)S(1)} %bitcast.255, bf16[1024,256]{1,0:T(8,128)(2,1)S(1)} %bitcast.252, bf16[]{:T(256)} %constant.13.clone.1), kind=kCustom, calls=%fused_computation.106 | custom fusion | bytes 524290 | tf_op jit(solution)/shard_map/scatter | solution.py:89
  (90 shorter events, 25.1 us)
Async XLA Ops:
  0.0 6.8 %copy-start = (bf16[2,512,512]{2,1,0:T(8,128)(2,1)S(1)}, bf16[2,512,512]{2,1,0:T(8,128)(2,1)}, u32[]{:S(2)}) copy-start(bf16[2,512,512]{2,1,0:T(8,128)(2,1)} %param.8) | copy-start | bytes 3145732
  0.8 5.3 %copy-start.25 = (s32[1,1024]{1,0:T(1,128)S(1)}, s32[1,1024]{1,0:T(1,128)}, u32[]{:S(2)}) copy-start(s32[1,1024]{1,0:T(1,128)} %param.7) | copy-start | bytes 12292
  6.8 1.0 copy-start.1
  7.9 1.3 copy-start.24
  17.8 24.9 %copy-start.3 = (bf16[512,256]{0,1:T(8,128)(2,1)}, bf16[512,256]{0,1:T(8,128)(2,1)S(1)}, u32[]{:S(2)}) copy-start(bf16[512,256]{0,1:T(8,128)(2,1)S(1)} %all-gather) | copy-start | bytes 786436
  23.4 24.0 %copy-start.5 = (bf16[512,256]{0,1:T(8,128)(2,1)}, bf16[512,256]{0,1:T(8,128)(2,1)S(1)}, u32[]{:S(2)}) copy-start(bf16[512,256]{0,1:T(8,128)(2,1)S(1)} %all-gather.1) | copy-start | bytes 786436
  33.4 20.2 %copy-start.7 = (bf16[512,256]{0,1:T(8,128)(2,1)}, bf16[512,256]{0,1:T(8,128)(2,1)S(1)}, u32[]{:S(2)}) copy-start(bf16[512,256]{0,1:T(8,128)(2,1)S(1)} %all-gather.2) | copy-start | bytes 786436
  42.7 15.6 %copy-start.9 = (bf16[512,256]{0,1:T(8,128)(2,1)}, bf16[512,256]{0,1:T(8,128)(2,1)S(1)}, u32[]{:S(2)}) copy-start(bf16[512,256]{0,1:T(8,128)(2,1)S(1)} %all-gather.3) | copy-start | bytes 786436
  47.4 17.7 %copy-start.11 = (bf16[512,256]{0,1:T(8,128)(2,1)}, bf16[512,256]{0,1:T(8,128)(2,1)S(1)}, u32[]{:S(2)}) copy-start(bf16[512,256]{0,1:T(8,128)(2,1)S(1)} %all-gather.4) | copy-start | bytes 786436
  53.6 11.7 %copy-start.13 = (bf16[512,256]{0,1:T(8,128)(2,1)}, bf16[512,256]{0,1:T(8,128)(2,1)S(1)}, u32[]{:S(2)}) copy-start(bf16[512,256]{0,1:T(8,128)(2,1)S(1)} %all-gather.5) | copy-start | bytes 786436
  53.6 12.2 %slice-start = ((bf16[1,9,256,256]{3,2,1,0:T(8,128)(2,1)}), bf16[1,1,256,256]{3,2,1,0:T(8,128)(2,1)S(1)}, s32[]{:S(2)}) async-start(bf16[1,9,256,256]{3,2,1,0:T(8,128)(2,1)} %param.11), calls=%async_computation | async-start | bytes 262144 | tf_op jit(solution)/shard_map/slice | solution.py:65
  58.4 7.0 %copy-start.15 = (bf16[512,256]{0,1:T(8,128)(2,1)}, bf16[512,256]{0,1:T(8,128)(2,1)S(1)}, u32[]{:S(2)}) copy-start(bf16[512,256]{0,1:T(8,128)(2,1)S(1)} %all-gather.6) | copy-start | bytes 786436
  65.1 0.7 copy-start.17
  66.1 14.2 %copy-start.18 = (bf16[512,256]{0,1:T(8,128)(2,1)S(1)}, bf16[512,256]{0,1:T(8,128)(2,1)}, u32[]{:S(2)}) copy-start(bf16[512,256]{0,1:T(8,128)(2,1)} %copy-done.17) | copy-start | bytes 786436
  78.8 2.7 %copy-start.2 = (bf16[1,9,256,256]{3,2,1,0:T(8,128)(2,1)S(1)}, bf16[1,9,256,256]{3,2,1,0:T(8,128)(2,1)}, u32[]{:S(2)}) copy-start(bf16[1,9,256,256]{3,2,1,0:T(8,128)(2,1)} %param.11) | copy-start | bytes 3538948
  78.8 15.2 %copy-start.16 = (bf16[512,256]{0,1:T(8,128)(2,1)S(1)}, bf16[512,256]{0,1:T(8,128)(2,1)}, u32[]{:S(2)}) copy-start(bf16[512,256]{0,1:T(8,128)(2,1)} %copy-done.15) | copy-start | bytes 786436
  81.5 0.7 copy-start.23
  82.2 19.0 %copy-start.14 = (bf16[512,256]{0,1:T(8,128)(2,1)S(1)}, bf16[512,256]{0,1:T(8,128)(2,1)}, u32[]{:S(2)}) copy-start(bf16[512,256]{0,1:T(8,128)(2,1)} %copy-done.13) | copy-start | bytes 786436
  96.4 14.0 %copy-start.12 = (bf16[512,256]{0,1:T(8,128)(2,1)S(1)}, bf16[512,256]{0,1:T(8,128)(2,1)}, u32[]{:S(2)}) copy-start(bf16[512,256]{0,1:T(8,128)(2,1)} %copy-done.11) | copy-start | bytes 786436
  102.4 0.7 copy-start.21
  104.2 14.1 %copy-start.10 = (bf16[512,256]{0,1:T(8,128)(2,1)S(1)}, bf16[512,256]{0,1:T(8,128)(2,1)}, u32[]{:S(2)}) copy-start(bf16[512,256]{0,1:T(8,128)(2,1)} %copy-done.9) | copy-start | bytes 786436
  113.5 15.8 %copy-start.8 = (bf16[512,256]{0,1:T(8,128)(2,1)S(1)}, bf16[512,256]{0,1:T(8,128)(2,1)}, u32[]{:S(2)}) copy-start(bf16[512,256]{0,1:T(8,128)(2,1)} %copy-done.7) | copy-start | bytes 786436
  120.7 17.4 %copy-start.6 = (bf16[512,256]{0,1:T(8,128)(2,1)S(1)}, bf16[512,256]{0,1:T(8,128)(2,1)}, u32[]{:S(2)}) copy-start(bf16[512,256]{0,1:T(8,128)(2,1)} %copy-done.5) | copy-start | bytes 786436
  132.4 16.3 %copy-start.4 = (bf16[512,256]{0,1:T(8,128)(2,1)S(1)}, bf16[512,256]{0,1:T(8,128)(2,1)}, u32[]{:S(2)}) copy-start(bf16[512,256]{0,1:T(8,128)(2,1)} %copy-done.3) | copy-start | bytes 786436
  (3 other events, 2.0 us)

commit v2 on v1

v2 whole, which is shorter than its diff:
```python
import functools

import functools

import jax
import jax.numpy as jnp
from jax import lax
from jax.experimental import pallas as pl
from jax.experimental.pallas import tpu as pltpu
from jax.sharding import PartitionSpec as P

BF16 = jnp.bfloat16
F32 = jnp.float32
MIB = 1 << 20


def pair_groups(size, bit):
    step = 1 << bit
    return [[i, i ^ step] for i in range(size) if not i & step]


def axis_of(level, col_bits):
    return ("col", level) if level < col_bits else ("row", level - col_bits)


def both(value, level, col_bits):
    axis, bit = axis_of(level, col_bits)
    groups = pair_groups(lax.axis_size(axis), bit)
    return lax.all_gather(value, axis, axis=0, tiled=False, axis_index_groups=groups)


def partner_slot(level, col_bits):
    axis, bit = axis_of(level, col_bits)
    return 1 - lax.rem(lax.div(lax.axis_index(axis), 1 << bit), 2)


def times(a, b):
    return jnp.dot(a, b, preferred_element_type=F32)


def times_transposed(a, b):
    return lax.dot_general(a, b, (((0,), (0,)), ((), ())), preferred_element_type=F32)


def pair_sum(pair_ref):
    return pair_ref[0].astype(F32) + pair_ref[1].astype(F32)


def call(kernel, outs, n_in, limit):
    vmem = [pl.BlockSpec(memory_space=pltpu.VMEM)] * n_in
    return pl.pallas_call(
        kernel,
        out_shape=[jax.ShapeDtypeStruct(shape, dtype) for shape, dtype in outs],
        in_specs=vmem,
        out_specs=[pl.BlockSpec(memory_space=pltpu.VMEM)] * len(outs),
        compiler_params=pltpu.CompilerParams(vmem_limit_bytes=limit),
    )


def leaf_kernel(order_ref, rhs_ref, inverse_ref, basis_ref, up_ref, rows_ref, state_ref, term_ref):
    rows = rhs_ref.shape[0]
    leaves, leaf = inverse_ref.shape[:2]
    across = jnp.broadcast_to(order_ref[...], (128, rows)).T
    lane = lax.broadcasted_iota(jnp.int32, (rows, 128), 1)
    pick = jnp.concatenate(
        [jnp.where(across == lane + 128 * b, 1.0, 0.0).astype(BF16) for b in range(rows // 128)],
        axis=1,
    )
    ordered = times(pick, rhs_ref[...]).astype(BF16)
    state = None
    for j in range(leaves):
        block = times(inverse_ref[j], ordered[j * leaf : (j + 1) * leaf])
        rows_ref[j] = block
        part = times_transposed(basis_ref[j], block.astype(BF16))
        state = part if state is None else state + part
    state_ref[...] = state
    term_ref[...] = times(up_ref[0, 0], state.astype(BF16)).astype(BF16)


def up_kernel(level, pair_ref, up_ref, term_ref):
    term_ref[...] = times(up_ref[0, level], pair_sum(pair_ref).astype(BF16)).astype(BF16)


def last_up_kernel(level, pair_ref, up_ref, down_ref, out_ref):
    out_ref[0] = times(up_ref[0, level], pair_sum(pair_ref).astype(BF16)).astype(BF16)
    out_ref[1] = down_ref[0, level]


def top_kernel(level, col_bits, pair_ref, saved_ref, up_ref, down_ref, y_ref, sent_ref):
    y = (pair_ref[0, 0].astype(F32) + pair_ref[1, 0].astype(F32)).astype(BF16)
    coupled = times(pair_ref[partner_slot(level, col_bits), 1], y).astype(BF16).astype(F32)
    top = pair_sum(saved_ref) + 0.5 * (coupled - times_transposed(up_ref[0, level], y))
    y_ref[...] = top.astype(BF16)
    sent_ref[...] = times(down_ref[0, level - 1], top.astype(BF16)).astype(BF16)


def down_kernel(level, col_bits, pair_ref, saved_ref, above_ref, up_ref, down_ref, y_ref, sent_ref):
    coupled = pair_ref[partner_slot(level, col_bits)].astype(F32)
    top = pair_sum(saved_ref) + 0.5 * (coupled - times_transposed(up_ref[0, level], above_ref[...]))
    y_ref[...] = top.astype(BF16)
    sent_ref[...] = times(down_ref[0, level - 1], top.astype(BF16)).astype(BF16)


def last_kernel(
    col_bits, order_ref, pair_ref, state_ref, above_ref, up_ref, inverse_ref, basis_ref, rows_ref, out_ref
):
    rows = out_ref.shape[0]
    leaves = inverse_ref.shape[0]
    coupled = pair_ref[partner_slot(0, col_bits)].astype(F32)
    top = state_ref[...] + 0.5 * (coupled - times_transposed(up_ref[0, 0], above_ref[...]))
    top_half = top.astype(BF16)
    solved = []
    for j in range(leaves):
        back = times(basis_ref[j], top_half).astype(BF16)
        solved.append((rows_ref[j] - times(inverse_ref[j], back)).astype(BF16))
    place = lax.broadcasted_iota(jnp.int32, (rows, rows), 0) == order_ref[...]
    pick = jnp.where(place, 1.0, 0.0).astype(BF16)
    out_ref[...] = times(pick, jnp.concatenate(solved, axis=0)).astype(BF16)


def on_device(
    rhs, order, leaf_inverse, leaf_column_generator, factor_up, downward_coupling_factors
):
    leaves, leaf = leaf_inverse.shape[:2]
    rank = leaf_column_generator.shape[2]
    genes = rhs.shape[1]
    levels = factor_up.shape[1]
    last = levels - 1
    col_bits = lax.axis_size("col").bit_length() - 1
    up, down = factor_up, downward_coupling_factors
    small = (rank, genes)
    steps = [(small, BF16), (small, BF16)]

    rows, state, term = call(
        leaf_kernel, [((leaves, leaf, genes), F32), (small, F32), (small, BF16)], 5, 24 * MIB
    )(order, rhs, leaf_inverse, leaf_column_generator, up)
    pairs = [both(term, 0, col_bits)]
    for level in range(1, last):
        (term,) = call(functools.partial(up_kernel, level), [(small, BF16)], 2, 4 * MIB)(pairs[-1], up)
        pairs.append(both(term, level, col_bits))
    (packed,) = call(functools.partial(last_up_kernel, last), [((2,) + small, BF16)], 3, 4 * MIB)(pairs[-1], up, down)
    y, sent = call(functools.partial(top_kernel, last, col_bits), steps, 4, 6 * MIB)(
        both(packed, last, col_bits), pairs[last - 1], up, down
    )
    for level in range(last - 1, 0, -1):
        y, sent = call(functools.partial(down_kernel, level, col_bits), steps, 5, 6 * MIB)(
            both(sent, level, col_bits), pairs[level - 1], y, up, down
        )
    (solved,) = call(functools.partial(last_kernel, col_bits), [(rhs.shape, BF16)], 8, 24 * MIB)(
        order, both(sent, 0, col_bits), state, y, up, leaf_inverse, leaf_column_generator, rows
    )
    return solved


def solution(mesh):
    in_specs = (
        P(("row", "col"), None),
        P(("row", "col"), None),
        P(("row", "col"), None, None),
        P(("row", "col"), None, None),
        P(("row", "col"), None, None, None),
        P(("row", "col"), None, None, None),
    )
    out_specs = P(("row", "col"), None)
    return jax.shard_map(
        on_device, mesh=mesh, in_specs=in_specs, out_specs=out_specs, check_vma=False
    )
```

time: 177 us -> 150 us (0.85)
  matrix products: 23.9 us -> 0 us
  local copies, waits for them, and re-layouts: 16.5 us -> 5.28 us
  Pallas kernels: 0 us -> 9.39 us
    dot_general x30 -> x0, matrix products: 23.9 us -> none  [the longest x18 11.5 us: times(): return jnp.dot(kernel_matrix, value, preferred_element_type=jnp.float32)]
    pallas_call x0 -> x18, Pallas kernels: none -> 9.39 us  [the longest x7 2.95 us: on_device(): call(functools.partial(down_kernel, level, col_bits), steps, 5, 6 * MIB)]
    scatter x1 -> x0, local copies, waits for them, and re-layouts: 5.72 us -> none  [on_device(): return placed.at[positions].set(flat)]
    gather x2 -> x0, local copies, waits for them, and re-layouts: 4.79 us -> none  [on_device(): ordered = jnp.take(rhs, positions, axis=0)]
    unnamed x54 -> x16, local copies, waits for them, and re-layouts: 5.69 us -> 5.28 us
where the time goes in v2:
time: 150 us
  blocking collectives  135 us (90%)
  Pallas kernels  9.39 us (6%)
  local copies, waits for them, and re-layouts  5.28 us (4%)
    all_gather x17, blocking collectives, both(): lax.all_gather(value, axis, axis=0, tiled=False, axis_index_groups=groups)  135 us
    unnamed x16, local copies, waits for them, and re-layouts  5.28 us

profile of v2, /device:TPU:1, one launch (start us, length us, event | category | flops | bytes accessed | tf_op | source)
XLA Modules:
  0.0 149.7 jit_solution(13015628554963320662)
XLA Ops:
  0.0 1.3 copy-done
  1.3 1.2 copy-done.3
  2.5 1.0 copy-done.5
  3.5 1.0 copy-done.6
  4.6 0.7 copy-done.7
  5.3 2.1 %shard_map.64 = (f32[2,512,256]{2,1,0:T(8,128)S(1)}, f32[256,256]{1,0:T(8,128)S(1)}, bf16[256,256]{1,0:T(8,128)(2,1)S(1)}) custom-call(s32[1,1024]{1,0:T(1,128)S(1)} %copy-done.7, bf16[1024,256]{1,0:T(8,128)(2,1)S(1)} %copy-done.6, bf16[2,512,512]{2,1,0:T(8,128)(2,1)S(1)} %copy-done.3, bf16[2,512,256]{2,1,0:T(8,128)(2,1)S(1)} %copy-done.5, ...), custom_call_target="tpu_custom_call" | custom-call | tf_op jit(solution)/shard_map/pallas_call | solution.py:134
  7.4 8.5 %all-gather = bf16[512,256]{1,0:T(8,128)(2,1)S(1)} all-gather(bf16[256,256]{1,0:T(8,128)(2,1)S(1)} %get-tuple-element.24), channel_id=2, replica_groups={{0,1},{2,3},{4,5},{6,7},{8,9},{10,11},{12,13},{14,15},{16,17},{18,19},{..., dimensions={0}, use_global_device_ids=true | all-gather | bytes 393216 | tf_op jit(solution)/shard_map/all_gather | solution.py:29
  16.1 5.4 %all-gather.1 = bf16[512,256]{1,0:T(8,128)(2,1)S(1)} all-gather(bf16[256,256]{1,0:T(8,128)(2,1)S(1)} %shard_map.65), channel_id=3, replica_groups={{0,2},{1,3},{4,6},{5,7},{8,10},{9,11},{12,14},{13,15},{16,18},{17,19},{..., dimensions={0}, use_global_device_ids=true | all-gather | bytes 393216 | tf_op jit(solution)/shard_map/all_gather | solution.py:29
  21.6 9.8 %all-gather.2 = bf16[512,256]{1,0:T(8,128)(2,1)S(1)} all-gather(bf16[256,256]{1,0:T(8,128)(2,1)S(1)} %shard_map.66), channel_id=4, replica_groups={{0,4},{1,5},{2,6},{3,7},{8,12},{9,13},{10,14},{11,15},{16,20},{17,21},{..., dimensions={0}, use_global_device_ids=true | all-gather | bytes 393216 | tf_op jit(solution)/shard_map/all_gather | solution.py:29
  31.6 9.0 %all-gather.3 = bf16[512,256]{1,0:T(8,128)(2,1)S(1)} all-gather(bf16[256,256]{1,0:T(8,128)(2,1)S(1)} %shard_map.67), channel_id=5, replica_groups={{0,8},{1,9},{2,10},{3,11},{4,12},{5,13},{6,14},{7,15},{16,24},{17,25},{..., dimensions={0}, use_global_device_ids=true | all-gather | bytes 393216 | tf_op jit(solution)/shard_map/all_gather | solution.py:29
  40.8 4.5 %all-gather.4 = bf16[512,256]{1,0:T(8,128)(2,1)S(1)} all-gather(bf16[256,256]{1,0:T(8,128)(2,1)S(1)} %shard_map.68), channel_id=6, replica_groups={{0,16},{32,48},{64,80},{96,112},{128,144},{160,176},{192,208},{224,240}..., dimensions={0}, use_global_device_ids=true | all-gather | bytes 393216 | tf_op jit(solution)/shard_map/all_gather | solution.py:29
  45.5 6.0 %all-gather.5 = bf16[512,256]{1,0:T(8,128)(2,1)S(1)} all-gather(bf16[256,256]{1,0:T(8,128)(2,1)S(1)} %shard_map.69), channel_id=7, replica_groups={{0,32},{16,48},{64,96},{80,112},{128,160},{144,176},{192,224},{208,240}..., dimensions={0}, use_global_device_ids=true | all-gather | bytes 393216 | tf_op jit(solution)/shard_map/all_gather | solution.py:29
  51.7 4.6 %all-gather.6 = bf16[512,256]{1,0:T(8,128)(2,1)S(1)} all-gather(bf16[256,256]{1,0:T(8,128)(2,1)S(1)} %shard_map.70), channel_id=8, replica_groups={{0,64},{16,80},{32,96},{48,112},{128,192},{144,208},{160,224},{176,240}..., dimensions={0}, use_global_device_ids=true | all-gather | bytes 393216 | tf_op jit(solution)/shard_map/all_gather | solution.py:29
  56.5 6.5 %all-gather.7 = bf16[512,256]{1,0:T(8,128)(2,1)S(1)} all-gather(bf16[256,256]{1,0:T(8,128)(2,1)S(1)} %shard_map.71), channel_id=9, replica_groups={{0,128},{16,144},{32,160},{48,176},{64,192},{80,208},{96,224},{112,240}..., dimensions={0}, use_global_device_ids=true | all-gather | bytes 393216 | tf_op jit(solution)/shard_map/all_gather | solution.py:29
  63.2 10.4 %all-gather.8 = bf16[4,256,256]{2,1,0:T(8,128)(2,1)S(1)} all-gather(bf16[2,256,256]{2,1,0:T(8,128)(2,1)S(1)} %shard_map.72), channel_id=10, replica_groups={{0,256},{16,272},{32,288},{48,304},{64,320},{80,336},{96,352},{112,368}..., dimensions={0}, use_global_device_ids=true | all-gather | bytes 786432 | tf_op jit(solution)/shard_map/all_gather | solution.py:29
  74.0 6.1 %all-gather.9 = bf16[512,256]{1,0:T(8,128)(2,1)S(1)} all-gather(bf16[256,256]{1,0:T(8,128)(2,1)S(1)} %get-tuple-element.25), channel_id=11, replica_groups={{0,128},{16,144},{32,160},{48,176},{64,192},{80,208},{96,224},{112,240}..., dimensions={0}, use_global_device_ids=true | all-gather | bytes 393216 | tf_op jit(solution)/shard_map/all_gather | solution.py:29
  80.5 9.5 %all-gather.10 = bf16[512,256]{1,0:T(8,128)(2,1)S(1)} all-gather(bf16[256,256]{1,0:T(8,128)(2,1)S(1)} %get-tuple-element.27), channel_id=12, replica_groups={{0,64},{16,80},{32,96},{48,112},{128,192},{144,208},{160,224},{176,240}..., dimensions={0}, use_global_device_ids=true | all-gather | bytes 393216 | tf_op jit(solution)/shard_map/all_gather | solution.py:29
  90.4 6.0 %all-gather.11 = bf16[512,256]{1,0:T(8,128)(2,1)S(1)} all-gather(bf16[256,256]{1,0:T(8,128)(2,1)S(1)} %get-tuple-element.29), channel_id=13, replica_groups={{0,32},{16,48},{64,96},{80,112},{128,160},{144,176},{192,224},{208,240}..., dimensions={0}, use_global_device_ids=true | all-gather | bytes 393216 | tf_op jit(solution)/shard_map/all_gather | solution.py:29
  96.8 7.5 %all-gather.12 = bf16[512,256]{1,0:T(8,128)(2,1)S(1)} all-gather(bf16[256,256]{1,0:T(8,128)(2,1)S(1)} %get-tuple-element.31), channel_id=14, replica_groups={{0,16},{32,48},{64,80},{96,112},{128,144},{160,176},{192,208},{224,240}..., dimensions={0}, use_global_device_ids=true | all-gather | bytes 393216 | tf_op jit(solution)/shard_map/all_gather | solution.py:29
  104.7 9.8 %all-gather.13 = bf16[512,256]{1,0:T(8,128)(2,1)S(1)} all-gather(bf16[256,256]{1,0:T(8,128)(2,1)S(1)} %get-tuple-element.33), channel_id=15, replica_groups={{0,8},{1,9},{2,10},{3,11},{4,12},{5,13},{6,14},{7,15},{16,24},{17,25},{..., dimensions={0}, use_global_device_ids=true | all-gather | bytes 393216 | tf_op jit(solution)/shard_map/all_gather | solution.py:29
  115.0 6.8 %all-gather.14 = bf16[512,256]{1,0:T(8,128)(2,1)S(1)} all-gather(bf16[256,256]{1,0:T(8,128)(2,1)S(1)} %get-tuple-element.35), channel_id=16, replica_groups={{0,4},{1,5},{2,6},{3,7},{8,12},{9,13},{10,14},{11,15},{16,20},{17,21},{..., dimensions={0}, use_global_device_ids=true | all-gather | bytes 393216 | tf_op jit(solution)/shard_map/all_gather | solution.py:29
  122.2 4.8 %all-gather.15 = bf16[512,256]{1,0:T(8,128)(2,1)S(1)} all-gather(bf16[256,256]{1,0:T(8,128)(2,1)S(1)} %get-tuple-element.37), channel_id=17, replica_groups={{0,2},{1,3},{4,6},{5,7},{8,10},{9,11},{12,14},{13,15},{16,18},{17,19},{..., dimensions={0}, use_global_device_ids=true | all-gather | bytes 393216 | tf_op jit(solution)/shard_map/all_gather | solution.py:29
  127.4 19.9 %all-gather.16 = bf16[512,256]{1,0:T(8,128)(2,1)S(1)} all-gather(bf16[256,256]{1,0:T(8,128)(2,1)S(1)} %get-tuple-element.39), channel_id=18, replica_groups={{0,1},{2,3},{4,5},{6,7},{8,9},{10,11},{12,13},{14,15},{16,17},{18,19},{..., dimensions={0}, use_global_device_ids=true | all-gather | bytes 393216 | tf_op jit(solution)/shard_map/all_gather | solution.py:29
  147.3 2.4 %shard_map.81 = bf16[1024,256]{1,0:T(8,128)(2,1)} custom-call(s32[1,1024]{1,0:T(1,128)S(1)} %copy-done.7, bf16[2,256,256]{2,1,0:T(8,128)(2,1)S(1)} %bitcast.41, f32[256,256]{1,0:T(8,128)S(1)} %get-tuple-element.40.state_ref, bf16[256,256]{1,0:T(8,128)(2,1)S(1)} %get-tuple-element.41.above_ref, bf16[1,9,256,256]{3,2,1,0:T(8,128)(2,1)S(1)} %copy-done.1, ...), custom_call_target="tpu_custom_call" | custom-call | tf_op jit(solution)/shard_map/pallas_call | solution.py:149
  (27 shorter events, 4.9 us)
Async XLA Ops:
  0.0 1.3 copy-start
  1.3 1.2 copy-start.3
  2.5 1.0 copy-start.5
  3.5 1.0 copy-start.6
  4.6 0.7 copy-start.7
  51.7 11.3 %copy-start.2 = (bf16[1,9,256,256]{3,2,1,0:T(8,128)(2,1)S(1)}, bf16[1,9,256,256]{3,2,1,0:T(8,128)(2,1)}, u32[]{:S(2)}) copy-start(bf16[1,9,256,256]{3,2,1,0:T(8,128)(2,1)} %down_ref.17) | copy-start | bytes 3538948
  127.0 20.4 %copy-start.1 = (bf16[1,9,256,256]{3,2,1,0:T(8,128)(2,1)S(1)}, bf16[1,9,256,256]{3,2,1,0:T(8,128)(2,1)}, u32[]{:S(2)}) copy-start(bf16[1,9,256,256]{3,2,1,0:T(8,128)(2,1)} %up_ref.35) | copy-start | bytes 3538948
  127.0 20.4 %copy-start.4 = (bf16[2,512,512]{2,1,0:T(8,128)(2,1)S(1)}, bf16[2,512,512]{2,1,0:T(8,128)(2,1)}, u32[]{:S(2)}) copy-start(bf16[2,512,512]{2,1,0:T(8,128)(2,1)} %inverse_ref.3) | copy-start | bytes 3145732

commit v3 on v2

--- a/solution.py
+++ b/solution.py
@@ -57,16 +57,37 @@
     )
 
 
-def leaf_kernel(order_ref, rhs_ref, inverse_ref, basis_ref, up_ref, rows_ref, state_ref, term_ref):
+def leaf_kernel(
+    order_hbm, rhs_hbm, inverse_hbm, basis_hbm, up_hbm, rows_ref, state_ref, term_ref,
+    order_ref, rhs_ref, inverse_ref, basis_ref, up_ref, sems,
+):
     rows = rhs_ref.shape[0]
     leaves, leaf = inverse_ref.shape[:2]
+    moves = [
+        pltpu.make_async_copy(src, dst, sems.at[k])
+        for k, (src, dst) in enumerate(
+            [
+                (order_hbm, order_ref),
+                (rhs_hbm, rhs_ref),
+                (inverse_hbm, inverse_ref),
+                (basis_hbm, basis_ref),
+                (up_hbm.at[0, 0], up_ref),
+            ]
+        )
+    ]
+    for move in moves:
+        move.start()
+    moves[0].wait()
     across = jnp.broadcast_to(order_ref[...], (128, rows)).T
     lane = lax.broadcasted_iota(jnp.int32, (rows, 128), 1)
     pick = jnp.concatenate(
         [jnp.where(across == lane + 128 * b, 1.0, 0.0).astype(BF16) for b in range(rows // 128)],
         axis=1,
     )
+    moves[1].wait()
     ordered = times(pick, rhs_ref[...]).astype(BF16)
+    moves[2].wait()
+    moves[3].wait()
     state = None
     for j in range(leaves):
         block = times(inverse_ref[j], ordered[j * leaf : (j + 1) * leaf])
@@ -74,7 +95,8 @@
         part = times_transposed(basis_ref[j], block.astype(BF16))
         state = part if state is None else state + part
     state_ref[...] = state
-    term_ref[...] = times(up_ref[0, 0], state.astype(BF16)).astype(BF16)
+    moves[4].wait()
+    term_ref[...] = times(up_ref[...], state.astype(BF16)).astype(BF16)
 
 
 def up_kernel(level, pair_ref, up_ref, term_ref):
@@ -131,8 +153,24 @@
     small = (rank, genes)
     steps = [(small, BF16), (small, BF16)]
 
-    rows, state, term = call(
-        leaf_kernel, [((leaves, leaf, genes), F32), (small, F32), (small, BF16)], 5, 24 * MIB
+    rows, state, term = pl.pallas_call(
+        leaf_kernel,
+        out_shape=[
+            jax.ShapeDtypeStruct((leaves, leaf, genes), F32),
+            jax.ShapeDtypeStruct(small, F32),
+            jax.ShapeDtypeStruct(small, BF16),
+        ],
+        in_specs=[pl.BlockSpec(memory_space=pltpu.HBM)] * 5,
+        out_specs=[pl.BlockSpec(memory_space=pltpu.VMEM)] * 3,
+        scratch_shapes=[
+            pltpu.VMEM(order.shape, order.dtype),
+            pltpu.VMEM(rhs.shape, BF16),
+            pltpu.VMEM(leaf_inverse.shape, BF16),
+            pltpu.VMEM(leaf_column_generator.shape, BF16),
+            pltpu.VMEM(factor_up.shape[2:], BF16),
+            pltpu.SemaphoreType.DMA((5,)),
+        ],
+        compiler_params=pltpu.CompilerParams(vmem_limit_bytes=56 * MIB),
     )(order, rhs, leaf_inverse, leaf_column_generator, up)
     pairs = [both(term, 0, col_bits)]
     for level in range(1, last):

time: 150 us -> 147 us (0.980)
  local copies, waits for them, and re-layouts: 5.28 us -> 0.03 us
  Pallas kernels: 9.39 us -> 11.8 us
    unnamed x16 -> x14, local copies, waits for them, and re-layouts: 5.28 us -> 0.03 us
    pallas_call x1, Pallas kernels: 2.12 us -> 4.59 us  [on_device(): pl.pallas_call(leaf_kernel, out_shape=[jax.ShapeDtypeStruct((leaves, leaf...]
where the time goes in v3:
time: 147 us
  blocking collectives  135 us (92%)
  Pallas kernels  11.8 us (8%)
    all_gather x17, blocking collectives, both(): lax.all_gather(value, axis, axis=0, tiled=False, axis_index_groups=groups)  135 us
    pallas_call x1, Pallas kernels, on_device(): pl.pallas_call(leaf_kernel, out_shape=[jax.ShapeDtypeStruct((leaves, leaf...  4.59 us

profile of v3, /device:TPU:1, one launch (start us, length us, event | category | flops | bytes accessed | tf_op | source)
XLA Modules:
  0.0 147.2 jit_solution(15740204641045647351)
XLA Ops:
  0.0 4.6 %shard_map.64 = (f32[2,512,256]{2,1,0:T(8,128)}, f32[256,256]{1,0:T(8,128)}, bf16[256,256]{1,0:T(8,128)(2,1)}) custom-call(s32[1,1024]{1,0:T(1,128)} %order_ref.1, bf16[1024,256]{1,0:T(8,128)(2,1)} %rhs_hbm.1, bf16[2,512,512]{2,1,0:T(8,128)(2,1)} %inverse_ref.1, bf16[2,512,256]{2,1,0:T(8,128)(2,1)} %basis_ref.1, bf16[1,9,256,256]{3,2,1,0:T(8,128)(2,1)} %up_ref.33), custom_call_target="tpu_custom_call" | custom-call | tf_op jit(solution)/shard_map/pallas_call | solution.py:156
  4.6 8.7 %all-gather = bf16[512,256]{1,0:T(8,128)(2,1)S(1)} all-gather(bf16[256,256]{1,0:T(8,128)(2,1)} %get-tuple-element.24), channel_id=2, replica_groups={{0,1},{2,3},{4,5},{6,7},{8,9},{10,11},{12,13},{14,15},{16,17},{18,19},{..., dimensions={0}, use_global_device_ids=true | all-gather | bytes 393216 | tf_op jit(solution)/shard_map/all_gather | solution.py:29
  13.5 5.3 %all-gather.1 = bf16[512,256]{1,0:T(8,128)(2,1)S(1)} all-gather(bf16[256,256]{1,0:T(8,128)(2,1)S(1)} %shard_map.65), channel_id=3, replica_groups={{0,2},{1,3},{4,6},{5,7},{8,10},{9,11},{12,14},{13,15},{16,18},{17,19},{..., dimensions={0}, use_global_device_ids=true | all-gather | bytes 393216 | tf_op jit(solution)/shard_map/all_gather | solution.py:29
  19.0 9.8 %all-gather.2 = bf16[512,256]{1,0:T(8,128)(2,1)S(1)} all-gather(bf16[256,256]{1,0:T(8,128)(2,1)S(1)} %shard_map.66), channel_id=4, replica_groups={{0,4},{1,5},{2,6},{3,7},{8,12},{9,13},{10,14},{11,15},{16,20},{17,21},{..., dimensions={0}, use_global_device_ids=true | all-gather | bytes 393216 | tf_op jit(solution)/shard_map/all_gather | solution.py:29
  29.0 9.0 %all-gather.3 = bf16[512,256]{1,0:T(8,128)(2,1)S(1)} all-gather(bf16[256,256]{1,0:T(8,128)(2,1)S(1)} %shard_map.67), channel_id=5, replica_groups={{0,8},{1,9},{2,10},{3,11},{4,12},{5,13},{6,14},{7,15},{16,24},{17,25},{..., dimensions={0}, use_global_device_ids=true | all-gather | bytes 393216 | tf_op jit(solution)/shard_map/all_gather | solution.py:29
  38.2 4.5 %all-gather.4 = bf16[512,256]{1,0:T(8,128)(2,1)S(1)} all-gather(bf16[256,256]{1,0:T(8,128)(2,1)S(1)} %shard_map.68), channel_id=6, replica_groups={{0,16},{32,48},{64,80},{96,112},{128,144},{160,176},{192,208},{224,240}..., dimensions={0}, use_global_device_ids=true | all-gather | bytes 393216 | tf_op jit(solution)/shard_map/all_gather | solution.py:29
  42.9 6.0 %all-gather.5 = bf16[512,256]{1,0:T(8,128)(2,1)S(1)} all-gather(bf16[256,256]{1,0:T(8,128)(2,1)S(1)} %shard_map.69), channel_id=7, replica_groups={{0,32},{16,48},{64,96},{80,112},{128,160},{144,176},{192,224},{208,240}..., dimensions={0}, use_global_device_ids=true | all-gather | bytes 393216 | tf_op jit(solution)/shard_map/all_gather | solution.py:29
  49.1 4.6 %all-gather.6 = bf16[512,256]{1,0:T(8,128)(2,1)S(1)} all-gather(bf16[256,256]{1,0:T(8,128)(2,1)S(1)} %shard_map.70), channel_id=8, replica_groups={{0,64},{16,80},{32,96},{48,112},{128,192},{144,208},{160,224},{176,240}..., dimensions={0}, use_global_device_ids=true | all-gather | bytes 393216 | tf_op jit(solution)/shard_map/all_gather | solution.py:29
  53.9 6.5 %all-gather.7 = bf16[512,256]{1,0:T(8,128)(2,1)S(1)} all-gather(bf16[256,256]{1,0:T(8,128)(2,1)S(1)} %shard_map.71), channel_id=9, replica_groups={{0,128},{16,144},{32,160},{48,176},{64,192},{80,208},{96,224},{112,240}..., dimensions={0}, use_global_device_ids=true | all-gather | bytes 393216 | tf_op jit(solution)/shard_map/all_gather | solution.py:29
  60.6 10.5 %all-gather.8 = bf16[4,256,256]{2,1,0:T(8,128)(2,1)S(1)} all-gather(bf16[2,256,256]{2,1,0:T(8,128)(2,1)S(1)} %shard_map.72), channel_id=10, replica_groups={{0,256},{16,272},{32,288},{48,304},{64,320},{80,336},{96,352},{112,368}..., dimensions={0}, use_global_device_ids=true | all-gather | bytes 786432 | tf_op jit(solution)/shard_map/all_gather | solution.py:29
  71.1 0.5 shard_map.73
  71.6 6.1 %all-gather.9 = bf16[512,256]{1,0:T(8,128)(2,1)S(1)} all-gather(bf16[256,256]{1,0:T(8,128)(2,1)S(1)} %get-tuple-element.25), channel_id=11, replica_groups={{0,128},{16,144},{32,160},{48,176},{64,192},{80,208},{96,224},{112,240}..., dimensions={0}, use_global_device_ids=true | all-gather | bytes 393216 | tf_op jit(solution)/shard_map/all_gather | solution.py:29
  77.7 0.4 shard_map.74
  78.1 9.3 %all-gather.10 = bf16[512,256]{1,0:T(8,128)(2,1)S(1)} all-gather(bf16[256,256]{1,0:T(8,128)(2,1)S(1)} %get-tuple-element.27), channel_id=12, replica_groups={{0,64},{16,80},{32,96},{48,112},{128,192},{144,208},{160,224},{176,240}..., dimensions={0}, use_global_device_ids=true | all-gather | bytes 393216 | tf_op jit(solution)/shard_map/all_gather | solution.py:29
  87.8 6.0 %all-gather.11 = bf16[512,256]{1,0:T(8,128)(2,1)S(1)} all-gather(bf16[256,256]{1,0:T(8,128)(2,1)S(1)} %get-tuple-element.29), channel_id=13, replica_groups={{0,32},{16,48},{64,96},{80,112},{128,160},{144,176},{192,224},{208,240}..., dimensions={0}, use_global_device_ids=true | all-gather | bytes 393216 | tf_op jit(solution)/shard_map/all_gather | solution.py:29
  93.8 0.4 shard_map.76
  94.2 7.4 %all-gather.12 = bf16[512,256]{1,0:T(8,128)(2,1)S(1)} all-gather(bf16[256,256]{1,0:T(8,128)(2,1)S(1)} %get-tuple-element.31), channel_id=14, replica_groups={{0,16},{32,48},{64,80},{96,112},{128,144},{160,176},{192,208},{224,240}..., dimensions={0}, use_global_device_ids=true | all-gather | bytes 393216 | tf_op jit(solution)/shard_map/all_gather | solution.py:29
  101.7 0.4 shard_map.77
  102.1 9.8 %all-gather.13 = bf16[512,256]{1,0:T(8,128)(2,1)S(1)} all-gather(bf16[256,256]{1,0:T(8,128)(2,1)S(1)} %get-tuple-element.33), channel_id=15, replica_groups={{0,8},{1,9},{2,10},{3,11},{4,12},{5,13},{6,14},{7,15},{16,24},{17,25},{..., dimensions={0}, use_global_device_ids=true | all-gather | bytes 393216 | tf_op jit(solution)/shard_map/all_gather | solution.py:29
  112.3 6.8 %all-gather.14 = bf16[512,256]{1,0:T(8,128)(2,1)S(1)} all-gather(bf16[256,256]{1,0:T(8,128)(2,1)S(1)} %get-tuple-element.35), channel_id=16, replica_groups={{0,4},{1,5},{2,6},{3,7},{8,12},{9,13},{10,14},{11,15},{16,20},{17,21},{..., dimensions={0}, use_global_device_ids=true | all-gather | bytes 393216 | tf_op jit(solution)/shard_map/all_gather | solution.py:29
  119.1 0.4 shard_map.79
  119.6 4.8 %all-gather.15 = bf16[512,256]{1,0:T(8,128)(2,1)S(1)} all-gather(bf16[256,256]{1,0:T(8,128)(2,1)S(1)} %get-tuple-element.37), channel_id=17, replica_groups={{0,2},{1,3},{4,6},{5,7},{8,10},{9,11},{12,14},{13,15},{16,18},{17,19},{..., dimensions={0}, use_global_device_ids=true | all-gather | bytes 393216 | tf_op jit(solution)/shard_map/all_gather | solution.py:29
  124.8 20.0 %all-gather.16 = bf16[512,256]{1,0:T(8,128)(2,1)S(1)} all-gather(bf16[256,256]{1,0:T(8,128)(2,1)S(1)} %get-tuple-element.39), channel_id=18, replica_groups={{0,1},{2,3},{4,5},{6,7},{8,9},{10,11},{12,13},{14,15},{16,17},{18,19},{..., dimensions={0}, use_global_device_ids=true | all-gather | bytes 393216 | tf_op jit(solution)/shard_map/all_gather | solution.py:29
  144.8 2.4 %shard_map.81 = bf16[1024,256]{1,0:T(8,128)(2,1)} custom-call(s32[1,1024]{1,0:T(1,128)S(1)} %copy-done.6, bf16[2,256,256]{2,1,0:T(8,128)(2,1)S(1)} %bitcast.41, f32[256,256]{1,0:T(8,128)S(1)} %copy-done.5, bf16[256,256]{1,0:T(8,128)(2,1)S(1)} %get-tuple-element.41.above_ref, bf16[1,9,256,256]{3,2,1,0:T(8,128)(2,1)S(1)} %copy-done, ...), custom_call_target="tpu_custom_call" | custom-call | tf_op jit(solution)/shard_map/pallas_call | solution.py:187
  (25 shorter events, 2.8 us)
Async XLA Ops:
  0.0 13.3 %copy-start = (bf16[1,9,256,256]{3,2,1,0:T(8,128)(2,1)S(1)}, bf16[1,9,256,256]{3,2,1,0:T(8,128)(2,1)}, u32[]{:S(2)}) copy-start(bf16[1,9,256,256]{3,2,1,0:T(8,128)(2,1)} %up_ref.33) | copy-start | bytes 3538948
  49.1 11.3 %copy-start.1 = (bf16[1,9,256,256]{3,2,1,0:T(8,128)(2,1)S(1)}, bf16[1,9,256,256]{3,2,1,0:T(8,128)(2,1)}, u32[]{:S(2)}) copy-start(bf16[1,9,256,256]{3,2,1,0:T(8,128)(2,1)} %down_ref.17) | copy-start | bytes 3538948
  124.3 20.4 %copy-start.2 = (bf16[2,512,512]{2,1,0:T(8,128)(2,1)S(1)}, bf16[2,512,512]{2,1,0:T(8,128)(2,1)}, u32[]{:S(2)}) copy-start(bf16[2,512,512]{2,1,0:T(8,128)(2,1)} %inverse_ref.1) | copy-start | bytes 3145732
  124.3 20.4 %copy-start.3 = (bf16[2,512,256]{2,1,0:T(8,128)(2,1)S(1)}, bf16[2,512,256]{2,1,0:T(8,128)(2,1)}, u32[]{:S(2)}) copy-start(bf16[2,512,256]{2,1,0:T(8,128)(2,1)} %basis_ref.1) | copy-start | bytes 1572868
  124.3 20.4 %copy-start.4 = (f32[2,512,256]{2,1,0:T(8,128)S(1)}, f32[2,512,256]{2,1,0:T(8,128)}, u32[]{:S(2)}) copy-start(f32[2,512,256]{2,1,0:T(8,128)} %get-tuple-element.42.rows_ref) | copy-start | bytes 3145732
  124.3 20.4 %copy-start.5 = (f32[256,256]{1,0:T(8,128)S(1)}, f32[256,256]{1,0:T(8,128)}, u32[]{:S(2)}) copy-start(f32[256,256]{1,0:T(8,128)} %get-tuple-element.40.state_ref) | copy-start | bytes 786436
  124.3 20.4 %copy-start.6 = (s32[1,1024]{1,0:T(1,128)S(1)}, s32[1,1024]{1,0:T(1,128)}, u32[]{:S(2)}) copy-start(s32[1,1024]{1,0:T(1,128)} %order_ref.1) | copy-start | bytes 12292

commit v4 on v3

--- a/solution.py
+++ b/solution.py
@@ -9,6 +9,7 @@
 from jax.experimental.pallas import tpu as pltpu
 from jax.sharding import PartitionSpec as P
 
+
 BF16 = jnp.bfloat16
 F32 = jnp.float32
 MIB = 1 << 20
@@ -27,6 +28,13 @@
     axis, bit = axis_of(level, col_bits)
     groups = pair_groups(lax.axis_size(axis), bit)
     return lax.all_gather(value, axis, axis=0, tiled=False, axis_index_groups=groups)
+
+
+def among_four(value, level, col_bits):
+    axis, bit = axis_of(level, col_bits)
+    step, size = 1 << bit, lax.axis_size(axis)
+    groups = [[i + step * k for k in range(4)] for i in range(size) if not i & (3 * step)]
+    return lax.all_to_all(value, axis, 0, 0, axis_index_groups=groups)
 
 
 def partner_slot(level, col_bits):
@@ -58,9 +66,10 @@
 
 
 def leaf_kernel(
-    order_hbm, rhs_hbm, inverse_hbm, basis_hbm, up_hbm, rows_ref, state_ref, term_ref,
-    order_ref, rhs_ref, inverse_ref, basis_ref, up_ref, sems,
+    order_hbm, rhs_hbm, inverse_hbm, basis_hbm, up_hbm, down_hbm, rows_ref, state_ref, term_ref, share_hbm,
+    order_ref, rhs_ref, inverse_ref, basis_ref, up_ref, share_ref, sems, share_sems,
 ):
+    last = up_hbm.shape[1] - 1
     rows = rhs_ref.shape[0]
     leaves, leaf = inverse_ref.shape[:2]
     moves = [
@@ -72,6 +81,9 @@
                 (inverse_hbm, inverse_ref),
                 (basis_hbm, basis_ref),
                 (up_hbm.at[0, 0], up_ref),
+                (up_hbm.at[0, last], share_ref.at[0]),
+                (down_hbm.at[0, last], share_ref.at[1]),
+                (down_hbm.at[0, last - 1], share_ref.at[2]),
             ]
         )
     ]
@@ -85,6 +97,14 @@
         axis=1,
     )
     moves[1].wait()
+    for move in moves[5:]:
+        move.wait()
+    spread = [
+        pltpu.make_async_copy(share_ref, share_hbm.at[k], share_sems.at[k])
+        for k in range(share_hbm.shape[0])
+    ]
+    for move in spread:
+        move.start()
     ordered = times(pick, rhs_ref[...]).astype(BF16)
     moves[2].wait()
     moves[3].wait()
@@ -97,23 +117,48 @@
     state_ref[...] = state
     moves[4].wait()
     term_ref[...] = times(up_ref[...], state.astype(BF16)).astype(BF16)
+    for move in spread:
+        move.wait()
 
 
 def up_kernel(level, pair_ref, up_ref, term_ref):
     term_ref[...] = times(up_ref[0, level], pair_sum(pair_ref).astype(BF16)).astype(BF16)
 
 
-def last_up_kernel(level, pair_ref, up_ref, down_ref, out_ref):
-    out_ref[0] = times(up_ref[0, level], pair_sum(pair_ref).astype(BF16)).astype(BF16)
-    out_ref[1] = down_ref[0, level]
-
-
-def top_kernel(level, col_bits, pair_ref, saved_ref, up_ref, down_ref, y_ref, sent_ref):
-    y = (pair_ref[0, 0].astype(F32) + pair_ref[1, 0].astype(F32)).astype(BF16)
-    coupled = times(pair_ref[partner_slot(level, col_bits), 1], y).astype(BF16).astype(F32)
-    top = pair_sum(saved_ref) + 0.5 * (coupled - times_transposed(up_ref[0, level], y))
-    y_ref[...] = top.astype(BF16)
-    sent_ref[...] = times(down_ref[0, level - 1], top.astype(BF16)).astype(BF16)
+def spread_kernel(level, pair_ref, up_ref, out_ref):
+    term = times(up_ref[0, level], pair_sum(pair_ref).astype(BF16)).astype(BF16)
+    for k in range(out_ref.shape[0]):
+        out_ref[k] = term
+
+
+def top_kernel(low, col_bits, terms_ref, share_ref, saved_ref, up_ref, down_ref, y_ref, sent_ref):
+    axis, bit = axis_of(low, col_bits)
+    me = lax.rem(lax.div(lax.axis_index(axis), 1 << bit), 4)
+    flip = 1 - 2 * lax.rem(me, 2)
+    across = 2 - 4 * lax.div(me, 2)
+    a, b, c, d = me, me + flip, me + across, me + flip + across
+
+    def rounded(x):
+        return x.astype(BF16)
+
+    def elim(member, value):
+        return rounded(times(share_ref[member, 0], value)).astype(F32)
+
+    def above(member, other, state, value):
+        coupled = rounded(times(share_ref[other, 1], value)).astype(F32)
+        return state + 0.5 * (coupled - times_transposed(share_ref[member, 0], value))
+
+    state = terms_ref[a].astype(F32) + terms_ref[b].astype(F32)
+    far = terms_ref[c].astype(F32) + terms_ref[d].astype(F32)
+    state_half, far_half = rounded(state), rounded(far)
+    y_mine = rounded(elim(a, state_half) + elim(c, far_half))
+    y_near = rounded(elim(b, state_half) + elim(d, far_half))
+    top_mine = rounded(above(a, c, state, y_mine))
+    top_near = rounded(above(b, d, state, y_near))
+    coupled = rounded(times(share_ref[b, 2], top_near)).astype(F32)
+    top = rounded(pair_sum(saved_ref) + 0.5 * (coupled - times_transposed(up_ref[0, low], top_mine)))
+    y_ref[...] = top
+    sent_ref[...] = rounded(times(down_ref[0, low - 1], top))
 
 
 def down_kernel(level, col_bits, pair_ref, saved_ref, above_ref, up_ref, down_ref, y_ref, sent_ref):
@@ -153,34 +198,41 @@
     small = (rank, genes)
     steps = [(small, BF16), (small, BF16)]
 
-    rows, state, term = pl.pallas_call(
+    rows, state, term, share = pl.pallas_call(
         leaf_kernel,
         out_shape=[
             jax.ShapeDtypeStruct((leaves, leaf, genes), F32),
             jax.ShapeDtypeStruct(small, F32),
             jax.ShapeDtypeStruct(small, BF16),
+            jax.ShapeDtypeStruct((4, 3) + factor_up.shape[2:], BF16),
         ],
-        in_specs=[pl.BlockSpec(memory_space=pltpu.HBM)] * 5,
-        out_specs=[pl.BlockSpec(memory_space=pltpu.VMEM)] * 3,
+        in_specs=[pl.BlockSpec(memory_space=pltpu.HBM)] * 6,
+        out_specs=[pl.BlockSpec(memory_space=pltpu.VMEM)] * 3 + [pl.BlockSpec(memory_space=pltpu.HBM)],
         scratch_shapes=[
             pltpu.VMEM(order.shape, order.dtype),
             pltpu.VMEM(rhs.shape, BF16),
             pltpu.VMEM(leaf_inverse.shape, BF16),
             pltpu.VMEM(leaf_column_generator.shape, BF16),
             pltpu.VMEM(factor_up.shape[2:], BF16),
-            pltpu.SemaphoreType.DMA((5,)),
+            pltpu.VMEM((3,) + factor_up.shape[2:], BF16),
+            pltpu.SemaphoreType.DMA((8,)),
+            pltpu.SemaphoreType.DMA((4,)),
         ],
         compiler_params=pltpu.CompilerParams(vmem_limit_bytes=56 * MIB),
-    )(order, rhs, leaf_inverse, leaf_column_generator, up)
+    )(order, rhs, leaf_inverse, leaf_column_generator, up, down)
     pairs = [both(term, 0, col_bits)]
-    for level in range(1, last):
+    low = last - 1
+    shared = among_four(share, low, col_bits)
+    for level in range(1, low):
         (term,) = call(functools.partial(up_kernel, level), [(small, BF16)], 2, 4 * MIB)(pairs[-1], up)
+        if level == low - 1:
+            term, shared = lax.optimization_barrier((term, shared))
         pairs.append(both(term, level, col_bits))
-    (packed,) = call(functools.partial(last_up_kernel, last), [((2,) + small, BF16)], 3, 4 * MIB)(pairs[-1], up, down)
-    y, sent = call(functools.partial(top_kernel, last, col_bits), steps, 4, 6 * MIB)(
-        both(packed, last, col_bits), pairs[last - 1], up, down
-    )
-    for level in range(last - 1, 0, -1):
+    (terms,) = call(functools.partial(spread_kernel, low), [((4,) + small, BF16)], 2, 4 * MIB)(pairs[-1], up)
+    y, sent = call(functools.partial(top_kernel, low, col_bits), steps, 5, 8 * MIB)(
+        among_four(terms, low, col_bits), shared, pairs[-1], up, down
+    )
+    for level in range(low - 1, 0, -1):
         y, sent = call(functools.partial(down_kernel, level, col_bits), steps, 5, 6 * MIB)(
             both(sent, level, col_bits), pairs[level - 1], y, up, down
         )
@@ -200,6 +252,5 @@
         P(("row", "col"), None, None, None),
     )
     out_specs = P(("row", "col"), None)
-    return jax.shard_map(
-        on_device, mesh=mesh, in_specs=in_specs, out_specs=out_specs, check_vma=False
-    )
+
+    return jax.shard_map(on_device, mesh=mesh, in_specs=in_specs, out_specs=out_specs, check_vma=False)

time: 147 us -> 141 us (0.959)
  blocking collectives: 135 us -> 115 us
  starting transfers between devices: 0 us -> 11 us
    all_gather x17 -> x14, blocking collectives: 135 us -> 96.5 us  [both(): lax.all_gather(value, axis, axis=0, tiled=False, axis_index_groups=groups)]
    all_to_all x0 -> x1, blocking collectives: none -> 18.6 us  [among_four(): return lax.all_to_all(value, axis, 0, 0, axis_index_groups=groups)]
    all_to_all x0 -> x1, starting transfers between devices: none -> 11 us  [among_four(): return lax.all_to_all(value, axis, 0, 0, axis_index_groups=groups)]
  transfers between devices with their start and end apart: 0 -> 1, of which waited for: 0 -> 0; matrix products, arithmetic and copies ran while one was open for 0% -> 0% of each run, Pallas kernels for 0% -> 1%
where the time goes in v4:
time: 141 us; the launch traced here: 140 us
  blocking collectives  115 us (82%)
  Pallas kernels  12.4 us (9%)
  starting transfers between devices  11 us (8%)
    all_gather x14, blocking collectives, both(): lax.all_gather(value, axis, axis=0, tiled=False, axis_index_groups=groups)  96.5 us
    all_to_all x1, blocking collectives, among_four(): return lax.all_to_all(value, axis, 0, 0, axis_index_groups=groups)  18.6 us
    all_to_all x1, starting transfers between devices, among_four(): return lax.all_to_all(value, axis, 0, 0, axis_index_groups=groups)  11 us
    pallas_call x1, Pallas kernels, on_device(): pl.pallas_call(leaf_kernel, out_shape=[jax.ShapeDtypeStruct((leaves, leaf...  5.24 us
  transfers between devices with their start and end apart: 1, of which 0 were waited for; matrix products, arithmetic and copies ran while one was open for 0% of the time, Pallas kernels for 1%

profile of v4, /device:TPU:1, one launch (start us, length us, event | category | flops | bytes accessed | tf_op | source)
XLA Modules:
  0.0 140.1 jit_solution(8927810983201964524)
XLA Ops:
  0.0 5.2 %shard_map.64 = (f32[2,512,256]{2,1,0:T(8,128)}, f32[256,256]{1,0:T(8,128)}, bf16[256,256]{1,0:T(8,128)(2,1)}, bf16[4,3,256,256]{3,2,1,0:T(8,128)(2,1)}) custom-call(s32[1,1024]{1,0:T(1,128)} %order_ref.1, bf16[1024,256]{1,0:T(8,128)(2,1)} %rhs_hbm.1, bf16[2,512,512]{2,1,0:T(8,128)(2,1)} %inverse_ref.1, bf16[2,512,256]{2,1,0:T(8,128)(2,1)} %basis_ref.1, ...), custom_call_target="tpu_custom_call" | custom-call | tf_op jit(solution)/shard_map/pallas_call | solution.py:201
  5.3 11.0 %all-to-all-start = ((bf16[4,3,256,256]{3,2,1,0:T(8,128)(2,1)}), bf16[4,3,256,256]{3,2,1,0:T(8,128)(2,1)S(1)}, u32[]{:S(2)}, u32[]{:S(2)}) async-start(bf16[4,3,256,256]{3,2,1,0:T(8,128)(2,1)} %get-tuple-element.26), calls=%async_computation | async-start | bytes 3145728 | tf_op jit(solution)/shard_map/all_to_all | solution.py:37
  16.3 2.6 %all-gather = bf16[512,256]{1,0:T(8,128)(2,1)S(1)} all-gather(bf16[256,256]{1,0:T(8,128)(2,1)S(1)} %copy-done.14), channel_id=2, replica_groups={{0,1},{2,3},{4,5},{6,7},{8,9},{10,11},{12,13},{14,15},{16,17},{18,19},{..., dimensions={0}, use_global_device_ids=true | all-gather | bytes 393216 | tf_op jit(solution)/shard_map/all_gather | solution.py:30
  19.0 5.3 %all-gather.1 = bf16[512,256]{1,0:T(8,128)(2,1)S(1)} all-gather(bf16[256,256]{1,0:T(8,128)(2,1)S(1)} %shard_map.65), channel_id=3, replica_groups={{0,2},{1,3},{4,6},{5,7},{8,10},{9,11},{12,14},{13,15},{16,18},{17,19},{..., dimensions={0}, use_global_device_ids=true | all-gather | bytes 393216 | tf_op jit(solution)/shard_map/all_gather | solution.py:30
  24.6 8.8 %all-gather.2 = bf16[512,256]{1,0:T(8,128)(2,1)S(1)} all-gather(bf16[256,256]{1,0:T(8,128)(2,1)S(1)} %shard_map.66), channel_id=4, replica_groups={{0,4},{1,5},{2,6},{3,7},{8,12},{9,13},{10,14},{11,15},{16,20},{17,21},{..., dimensions={0}, use_global_device_ids=true | all-gather | bytes 393216 | tf_op jit(solution)/shard_map/all_gather | solution.py:30
  33.5 10.1 %all-gather.3 = bf16[512,256]{1,0:T(8,128)(2,1)S(1)} all-gather(bf16[256,256]{1,0:T(8,128)(2,1)S(1)} %shard_map.67), channel_id=5, replica_groups={{0,8},{1,9},{2,10},{3,11},{4,12},{5,13},{6,14},{7,15},{16,24},{17,25},{..., dimensions={0}, use_global_device_ids=true | all-gather | bytes 393216 | tf_op jit(solution)/shard_map/all_gather | solution.py:30
  43.9 4.5 %all-gather.4 = bf16[512,256]{1,0:T(8,128)(2,1)S(1)} all-gather(bf16[256,256]{1,0:T(8,128)(2,1)S(1)} %shard_map.68), channel_id=6, replica_groups={{0,16},{32,48},{64,80},{96,112},{128,144},{160,176},{192,208},{224,240}..., dimensions={0}, use_global_device_ids=true | all-gather | bytes 393216 | tf_op jit(solution)/shard_map/all_gather | solution.py:30
  48.6 6.7 %all-gather.5 = bf16[512,256]{1,0:T(8,128)(2,1)S(1)} all-gather(bf16[256,256]{1,0:T(8,128)(2,1)S(1)} %shard_map.69), channel_id=7, replica_groups={{0,32},{16,48},{64,96},{80,112},{128,160},{144,176},{192,224},{208,240}..., dimensions={0}, use_global_device_ids=true | all-gather | bytes 393216 | tf_op jit(solution)/shard_map/all_gather | solution.py:30
  55.5 0.7 copy-done.7
  56.2 0.6 copy-done.11
  56.8 5.0 %all-gather.6 = bf16[512,256]{1,0:T(8,128)(2,1)S(1)} all-gather(bf16[256,256]{1,0:T(8,128)(2,1)} %copy-done.11), channel_id=8, replica_groups={{0,64},{16,80},{32,96},{48,112},{128,192},{144,208},{160,224},{176,240}..., dimensions={0}, use_global_device_ids=true | all-gather | bytes 393216 | tf_op jit(solution)/shard_map/all_gather | solution.py:30
  62.0 18.6 %all_to_all.10.terms_ref = bf16[4,256,256]{2,1,0:T(8,128)(2,1)S(1)} all-to-all(bf16[4,256,256]{2,1,0:T(8,128)(2,1)S(1)} %shard_map.71), channel_id=1, replica_groups={{0,128,256,384},{16,144,272,400},{32,160,288,416},{48,176,304,432},{64,..., dimensions={0} | all-to-all | bytes 1048576 | tf_op jit(solution)/shard_map/all_to_all | solution.py:37
  80.7 0.9 shard_map.72
  81.6 4.9 %all-gather.7 = bf16[512,256]{1,0:T(8,128)(2,1)S(1)} all-gather(bf16[256,256]{1,0:T(8,128)(2,1)S(1)} %get-tuple-element.29), channel_id=9, replica_groups={{0,64},{16,80},{32,96},{48,112},{128,192},{144,208},{160,224},{176,240}..., dimensions={0}, use_global_device_ids=true | all-gather | bytes 393216 | tf_op jit(solution)/shard_map/all_gather | solution.py:30
  86.5 0.4 shard_map.73
  86.9 6.0 %all-gather.8 = bf16[512,256]{1,0:T(8,128)(2,1)S(1)} all-gather(bf16[256,256]{1,0:T(8,128)(2,1)S(1)} %get-tuple-element.31), channel_id=10, replica_groups={{0,32},{16,48},{64,96},{80,112},{128,160},{144,176},{192,224},{208,240}..., dimensions={0}, use_global_device_ids=true | all-gather | bytes 393216 | tf_op jit(solution)/shard_map/all_gather | solution.py:30
  92.9 0.4 shard_map.74
  93.3 4.5 %all-gather.9 = bf16[512,256]{1,0:T(8,128)(2,1)S(1)} all-gather(bf16[256,256]{1,0:T(8,128)(2,1)S(1)} %get-tuple-element.33), channel_id=11, replica_groups={{0,16},{32,48},{64,80},{96,112},{128,144},{160,176},{192,208},{224,240}..., dimensions={0}, use_global_device_ids=true | all-gather | bytes 393216 | tf_op jit(solution)/shard_map/all_gather | solution.py:30
  98.2 9.8 %all-gather.10 = bf16[512,256]{1,0:T(8,128)(2,1)S(1)} all-gather(bf16[256,256]{1,0:T(8,128)(2,1)S(1)} %get-tuple-element.35), channel_id=12, replica_groups={{0,8},{1,9},{2,10},{3,11},{4,12},{5,13},{6,14},{7,15},{16,24},{17,25},{..., dimensions={0}, use_global_device_ids=true | all-gather | bytes 393216 | tf_op jit(solution)/shard_map/all_gather | solution.py:30
  108.5 6.0 %all-gather.11 = bf16[512,256]{1,0:T(8,128)(2,1)S(1)} all-gather(bf16[256,256]{1,0:T(8,128)(2,1)S(1)} %get-tuple-element.37), channel_id=13, replica_groups={{0,4},{1,5},{2,6},{3,7},{8,12},{9,13},{10,14},{11,15},{16,20},{17,21},{..., dimensions={0}, use_global_device_ids=true | all-gather | bytes 393216 | tf_op jit(solution)/shard_map/all_gather | solution.py:30
  114.9 6.8 %all-gather.12 = bf16[512,256]{1,0:T(8,128)(2,1)S(1)} all-gather(bf16[256,256]{1,0:T(8,128)(2,1)S(1)} %get-tuple-element.39), channel_id=14, replica_groups={{0,2},{1,3},{4,6},{5,7},{8,10},{9,11},{12,14},{13,15},{16,18},{17,19},{..., dimensions={0}, use_global_device_ids=true | all-gather | bytes 393216 | tf_op jit(solution)/shard_map/all_gather | solution.py:30
  121.7 0.4 shard_map.78
  122.2 15.6 %all-gather.13 = bf16[512,256]{1,0:T(8,128)(2,1)S(1)} all-gather(bf16[256,256]{1,0:T(8,128)(2,1)S(1)} %get-tuple-element.41), channel_id=15, replica_groups={{0,1},{2,3},{4,5},{6,7},{8,9},{10,11},{12,13},{14,15},{16,17},{18,19},{..., dimensions={0}, use_global_device_ids=true | all-gather | bytes 393216 | tf_op jit(solution)/shard_map/all_gather | solution.py:30
  137.7 2.4 %shard_map.79 = bf16[1024,256]{1,0:T(8,128)(2,1)} custom-call(s32[1,1024]{1,0:T(1,128)S(1)} %copy-done.13, bf16[2,256,256]{2,1,0:T(8,128)(2,1)S(1)} %bitcast.34, f32[256,256]{1,0:T(8,128)S(1)} %copy-done.12, bf16[256,256]{1,0:T(8,128)(2,1)S(1)} %get-tuple-element.43.above_ref, bf16[1,9,256,256]{3,2,1,0:T(8,128)(2,1)S(1)} %copy-done, ...), custom_call_target="tpu_custom_call" | custom-call | tf_op jit(solution)/shard_map/pallas_call | solution.py:239
  (39 shorter events, 2.6 us)
Async XLA Ops:
  5.2 11.0 %copy-start.14 = (bf16[256,256]{1,0:T(8,128)(2,1)S(1)}, bf16[256,256]{1,0:T(8,128)(2,1)}, u32[]{:S(2)}) copy-start(bf16[256,256]{1,0:T(8,128)(2,1)} %get-tuple-element.25) | copy-start | bytes 393220
  5.3 13.6 %copy-start = (bf16[1,9,256,256]{3,2,1,0:T(8,128)(2,1)S(1)}, bf16[1,9,256,256]{3,2,1,0:T(8,128)(2,1)}, u32[]{:S(2)}) copy-start(bf16[1,9,256,256]{3,2,1,0:T(8,128)(2,1)} %up_ref.29) | copy-start | bytes 3538948
  5.3 51.6 %all-to-all-start = ((bf16[4,3,256,256]{3,2,1,0:T(8,128)(2,1)}), bf16[4,3,256,256]{3,2,1,0:T(8,128)(2,1)S(1)}, u32[]{:S(2)}, u32[]{:S(2)}) async-start(bf16[4,3,256,256]{3,2,1,0:T(8,128)(2,1)} %get-tuple-element.26), calls=%async_computation | async-start | bytes 3145728 | tf_op jit(solution)/shard_map/all_to_all | solution.py:37
  43.7 4.9 %copy-start.3 = (bf16[512,256]{1,0:T(8,128)(2,1)}, bf16[512,256]{1,0:T(8,128)(2,1)S(1)}, u32[]{:S(2)}) copy-start(bf16[512,256]{1,0:T(8,128)(2,1)S(1)} %all-gather.3) | copy-start | bytes 786436
  48.4 6.9 %copy-start.5 = (bf16[512,256]{1,0:T(8,128)(2,1)}, bf16[512,256]{1,0:T(8,128)(2,1)S(1)}, u32[]{:S(2)}) copy-start(bf16[512,256]{1,0:T(8,128)(2,1)S(1)} %all-gather.4) | copy-start | bytes 786436
  55.5 0.7 copy-start.7
  56.2 0.6 copy-start.11
  61.8 18.8 %copy-start.1 = (bf16[1,9,256,256]{3,2,1,0:T(8,128)(2,1)S(1)}, bf16[1,9,256,256]{3,2,1,0:T(8,128)(2,1)}, u32[]{:S(2)}) copy-start(bf16[1,9,256,256]{3,2,1,0:T(8,128)(2,1)} %down_ref.13) | copy-start | bytes 3538948
  80.7 5.8 %copy-start.8 = (bf16[512,256]{1,0:T(8,128)(2,1)S(1)}, bf16[512,256]{1,0:T(8,128)(2,1)}, u32[]{:S(2)}) copy-start(bf16[512,256]{1,0:T(8,128)(2,1)} %copy-done.7) | copy-start | bytes 786436
  86.5 6.4 %copy-start.6 = (bf16[512,256]{1,0:T(8,128)(2,1)S(1)}, bf16[512,256]{1,0:T(8,128)(2,1)}, u32[]{:S(2)}) copy-start(bf16[512,256]{1,0:T(8,128)(2,1)} %copy-done.5) | copy-start | bytes 786436
  92.9 4.9 %copy-start.4 = (bf16[512,256]{1,0:T(8,128)(2,1)S(1)}, bf16[512,256]{1,0:T(8,128)(2,1)}, u32[]{:S(2)}) copy-start(bf16[512,256]{1,0:T(8,128)(2,1)} %copy-done.3) | copy-start | bytes 786436
  121.7 16.0 %copy-start.2 = (bf16[2,512,512]{2,1,0:T(8,128)(2,1)S(1)}, bf16[2,512,512]{2,1,0:T(8,128)(2,1)}, u32[]{:S(2)}) copy-start(bf16[2,512,512]{2,1,0:T(8,128)(2,1)} %inverse_ref.1) | copy-start | bytes 3145732
  121.7 16.0 %copy-start.9 = (bf16[2,512,256]{2,1,0:T(8,128)(2,1)S(1)}, bf16[2,512,256]{2,1,0:T(8,128)(2,1)}, u32[]{:S(2)}) copy-start(bf16[2,512,256]{2,1,0:T(8,128)(2,1)} %basis_ref.1) | copy-start | bytes 1572868
  121.7 16.0 %copy-start.10 = (f32[2,512,256]{2,1,0:T(8,128)S(1)}, f32[2,512,256]{2,1,0:T(8,128)}, u32[]{:S(2)}) copy-start(f32[2,512,256]{2,1,0:T(8,128)} %get-tuple-element.44.rows_ref) | copy-start | bytes 3145732
  121.7 16.0 %copy-start.12 = (f32[256,256]{1,0:T(8,128)S(1)}, f32[256,256]{1,0:T(8,128)}, u32[]{:S(2)}) copy-start(f32[256,256]{1,0:T(8,128)} %get-tuple-element.42.state_ref) | copy-start | bytes 786436
  121.7 16.0 %copy-start.13 = (s32[1,1024]{1,0:T(1,128)S(1)}, s32[1,1024]{1,0:T(1,128)}, u32[]{:S(2)}) copy-start(s32[1,1024]{1,0:T(1,128)} %order_ref.1) | copy-start | bytes 12292

commit v5 on v4

--- a/solution.py
+++ b/solution.py
@@ -35,6 +35,15 @@
     step, size = 1 << bit, lax.axis_size(axis)
     groups = [[i + step * k for k in range(4)] for i in range(size) if not i & (3 * step)]
     return lax.all_to_all(value, axis, 0, 0, axis_index_groups=groups)
+
+
+def group_index(level, col_bits):
+    axis, bit = axis_of(level, col_bits)
+    return lax.rem(lax.div(lax.axis_index(axis), 1 << bit), 4)
+
+
+def toggle(index, step):
+    return step - 2 * step * lax.rem(lax.div(index, step), 2)
 
 
 def partner_slot(level, col_bits):
@@ -66,10 +75,11 @@
 
 
 def leaf_kernel(
-    order_hbm, rhs_hbm, inverse_hbm, basis_hbm, up_hbm, down_hbm, rows_ref, state_ref, term_ref, share_hbm,
-    order_ref, rhs_ref, inverse_ref, basis_ref, up_ref, share_ref, sems, share_sems,
+    low, col_bits, order_hbm, rhs_hbm, inverse_hbm, basis_hbm, up_hbm, down_hbm, rows_hbm, state_hbm, term_ref, share_hbm,
+    order_ref, rhs_ref, inverse_ref, basis_ref, up_ref, share_ref, rows_ref, state_ref, sems, share_sems, out_sems,
 ):
     last = up_hbm.shape[1] - 1
+    me = group_index(low, col_bits)
     rows = rhs_ref.shape[0]
     leaves, leaf = inverse_ref.shape[:2]
     moves = [
@@ -81,43 +91,49 @@
                 (inverse_hbm, inverse_ref),
                 (basis_hbm, basis_ref),
                 (up_hbm.at[0, 0], up_ref),
-                (up_hbm.at[0, last], share_ref.at[0]),
-                (down_hbm.at[0, last], share_ref.at[1]),
-                (down_hbm.at[0, last - 1], share_ref.at[2]),
+                (down_hbm.at[0, last - 1], share_ref.at[0]),
+                (up_hbm.at[0, last], share_ref.at[1]),
+                (down_hbm.at[0, last], share_ref.at[2]),
             ]
         )
     ]
     for move in moves:
         move.start()
     moves[0].wait()
-    across = jnp.broadcast_to(order_ref[...], (128, rows)).T
-    lane = lax.broadcasted_iota(jnp.int32, (rows, 128), 1)
+    across = jnp.broadcast_to(order_ref[...], (128, rows)).T.astype(jnp.int16)
+    lane = lax.broadcasted_iota(jnp.int16, (rows, 128), 1)
     pick = jnp.concatenate(
-        [jnp.where(across == lane + 128 * b, 1.0, 0.0).astype(BF16) for b in range(rows // 128)],
+        [jnp.where(across == lane + jnp.int16(128 * b), BF16(1), BF16(0)) for b in range(rows // 128)],
         axis=1,
     )
     moves[1].wait()
+    ordered = times(pick, rhs_ref[...]).astype(BF16)
+    moves[2].wait()
+    moves[3].wait()
     for move in moves[5:]:
         move.wait()
+    near, across_pair = me + toggle(me, 1), me + toggle(me, 2)
+    slots = [(near, 0), (across_pair, 1), (near + across_pair - me, 1), (me, 1)]
     spread = [
-        pltpu.make_async_copy(share_ref, share_hbm.at[k], share_sems.at[k])
-        for k in range(share_hbm.shape[0])
+        pltpu.make_async_copy(share_ref.at[first : first + 2], share_hbm.at[slot], share_sems.at[k])
+        for k, (slot, first) in enumerate(slots)
     ]
     for move in spread:
         move.start()
-    ordered = times(pick, rhs_ref[...]).astype(BF16)
-    moves[2].wait()
-    moves[3].wait()
-    state = None
+    state, keep = None, []
     for j in range(leaves):
         block = times(inverse_ref[j], ordered[j * leaf : (j + 1) * leaf])
         rows_ref[j] = block
+        keep.append(pltpu.make_async_copy(rows_ref.at[j], rows_hbm.at[j], out_sems.at[j]))
+        keep[-1].start()
         part = times_transposed(basis_ref[j], block.astype(BF16))
         state = part if state is None else state + part
     state_ref[...] = state
+    keep.append(pltpu.make_async_copy(state_ref, state_hbm, out_sems.at[leaves]))
+    keep[-1].start()
     moves[4].wait()
     term_ref[...] = times(up_ref[...], state.astype(BF16)).astype(BF16)
-    for move in spread:
+    for move in spread + keep:
         move.wait()
 
 
@@ -132,30 +148,29 @@
 
 
 def top_kernel(low, col_bits, terms_ref, share_ref, saved_ref, up_ref, down_ref, y_ref, sent_ref):
-    axis, bit = axis_of(low, col_bits)
-    me = lax.rem(lax.div(lax.axis_index(axis), 1 << bit), 4)
-    flip = 1 - 2 * lax.rem(me, 2)
-    across = 2 - 4 * lax.div(me, 2)
+    me = group_index(low, col_bits)
+    flip, across = toggle(me, 1), toggle(me, 2)
     a, b, c, d = me, me + flip, me + across, me + flip + across
 
     def rounded(x):
         return x.astype(BF16)
 
-    def elim(member, value):
-        return rounded(times(share_ref[member, 0], value)).astype(F32)
-
-    def above(member, other, state, value):
-        coupled = rounded(times(share_ref[other, 1], value)).astype(F32)
-        return state + 0.5 * (coupled - times_transposed(share_ref[member, 0], value))
-
+    def elim(factor, value):
+        return rounded(times(factor, value)).astype(F32)
+
+    def above(factor, coupling, state, value):
+        coupled = rounded(times(coupling, value)).astype(F32)
+        return rounded(state + 0.5 * (coupled - times_transposed(factor, value)))
+
+    mine, near = up_ref[0, low + 1], share_ref[b, 1]
     state = terms_ref[a].astype(F32) + terms_ref[b].astype(F32)
     far = terms_ref[c].astype(F32) + terms_ref[d].astype(F32)
     state_half, far_half = rounded(state), rounded(far)
-    y_mine = rounded(elim(a, state_half) + elim(c, far_half))
-    y_near = rounded(elim(b, state_half) + elim(d, far_half))
-    top_mine = rounded(above(a, c, state, y_mine))
-    top_near = rounded(above(b, d, state, y_near))
-    coupled = rounded(times(share_ref[b, 2], top_near)).astype(F32)
+    y_mine = rounded(elim(mine, state_half) + elim(share_ref[c, 0], far_half))
+    y_near = rounded(elim(near, state_half) + elim(share_ref[d, 0], far_half))
+    top_mine = above(mine, share_ref[c, 1], state, y_mine)
+    top_near = above(near, share_ref[d, 1], state, y_near)
+    coupled = rounded(times(share_ref[b, 0], top_near)).astype(F32)
     top = rounded(pair_sum(saved_ref) + 0.5 * (coupled - times_transposed(up_ref[0, low], top_mine)))
     y_ref[...] = top
     sent_ref[...] = rounded(times(down_ref[0, low - 1], top))
@@ -180,8 +195,8 @@
     for j in range(leaves):
         back = times(basis_ref[j], top_half).astype(BF16)
         solved.append((rows_ref[j] - times(inverse_ref[j], back)).astype(BF16))
-    place = lax.broadcasted_iota(jnp.int32, (rows, rows), 0) == order_ref[...]
-    pick = jnp.where(place, 1.0, 0.0).astype(BF16)
+    place = lax.broadcasted_iota(jnp.int16, (rows, rows), 0) == order_ref[...].astype(jnp.int16)
+    pick = jnp.where(place, BF16(1), BF16(0))
     out_ref[...] = times(pick, jnp.concatenate(solved, axis=0)).astype(BF16)
 
 
@@ -193,21 +208,22 @@
     genes = rhs.shape[1]
     levels = factor_up.shape[1]
     last = levels - 1
+    low = last - 1
     col_bits = lax.axis_size("col").bit_length() - 1
     up, down = factor_up, downward_coupling_factors
     small = (rank, genes)
     steps = [(small, BF16), (small, BF16)]
 
     rows, state, term, share = pl.pallas_call(
-        leaf_kernel,
+        functools.partial(leaf_kernel, low, col_bits),
         out_shape=[
             jax.ShapeDtypeStruct((leaves, leaf, genes), F32),
             jax.ShapeDtypeStruct(small, F32),
             jax.ShapeDtypeStruct(small, BF16),
-            jax.ShapeDtypeStruct((4, 3) + factor_up.shape[2:], BF16),
+            jax.ShapeDtypeStruct((4, 2) + factor_up.shape[2:], BF16),
         ],
         in_specs=[pl.BlockSpec(memory_space=pltpu.HBM)] * 6,
-        out_specs=[pl.BlockSpec(memory_space=pltpu.VMEM)] * 3 + [pl.BlockSpec(memory_space=pltpu.HBM)],
+        out_specs=[pl.BlockSpec(memory_space=pltpu.VMEM if k == 2 else pltpu.HBM) for k in range(4)],
         scratch_shapes=[
             pltpu.VMEM(order.shape, order.dtype),
             pltpu.VMEM(rhs.shape, BF16),
@@ -215,19 +231,21 @@
             pltpu.VMEM(leaf_column_generator.shape, BF16),
             pltpu.VMEM(factor_up.shape[2:], BF16),
             pltpu.VMEM((3,) + factor_up.shape[2:], BF16),
+            pltpu.VMEM((leaves, leaf, genes), F32),
+            pltpu.VMEM(small, F32),
             pltpu.SemaphoreType.DMA((8,)),
             pltpu.SemaphoreType.DMA((4,)),
+            pltpu.SemaphoreType.DMA((leaves + 1,)),
         ],
         compiler_params=pltpu.CompilerParams(vmem_limit_bytes=56 * MIB),
     )(order, rhs, leaf_inverse, leaf_column_generator, up, down)
     pairs = [both(term, 0, col_bits)]
-    low = last - 1
     shared = among_four(share, low, col_bits)
     for level in range(1, low):
         (term,) = call(functools.partial(up_kernel, level), [(small, BF16)], 2, 4 * MIB)(pairs[-1], up)
+        pairs.append(both(term, level, col_bits))
         if level == low - 1:
-            term, shared = lax.optimization_barrier((term, shared))
-        pairs.append(both(term, level, col_bits))
+            pairs[-1], shared = lax.optimization_barrier((pairs[-1], shared))
     (terms,) = call(functools.partial(spread_kernel, low), [((4,) + small, BF16)], 2, 4 * MIB)(pairs[-1], up)
     y, sent = call(functools.partial(top_kernel, low, col_bits), steps, 5, 8 * MIB)(
         among_four(terms, low, col_bits), shared, pairs[-1], up, down

time: 141 us -> 139 us (0.986)
  no operation moved by 1% of the time
where the time goes in v5:
time: 139 us
  blocking collectives  115 us (83%)
  Pallas kernels  11.9 us (9%)
  starting transfers between devices  11 us (8%)
    all_gather x14, blocking collectives, both(): lax.all_gather(value, axis, axis=0, tiled=False, axis_index_groups=groups)  96.5 us
    all_to_all x1, blocking collectives, among_four(): return lax.all_to_all(value, axis, 0, 0, axis_index_groups=groups)  18.6 us
    all_to_all x1, starting transfers between devices, among_four(): return lax.all_to_all(value, axis, 0, 0, axis_index_groups=groups)  11 us
    pallas_call x1, Pallas kernels, on_device(): pl.pallas_call(functools.partial(leaf_kernel, low, col_bits), out_shape=[...  4.71 us
  transfers between devices with their start and end apart: 1, of which 0 were waited for; matrix products, arithmetic and copies ran while one was open for 0% of the time, Pallas kernels for 1%

profile of v5, /device:TPU:1, one launch (start us, length us, event | category | flops | bytes accessed | tf_op | source)
XLA Modules:
  0.0 138.7 jit_solution(112552768379757822)
XLA Ops:
  0.0 4.7 %shard_map.64 = (f32[2,512,256]{2,1,0:T(8,128)}, f32[256,256]{1,0:T(8,128)}, bf16[256,256]{1,0:T(8,128)(2,1)}, bf16[4,2,256,256]{3,2,1,0:T(8,128)(2,1)}) custom-call(s32[1,1024]{1,0:T(1,128)} %order_ref.1, bf16[1024,256]{1,0:T(8,128)(2,1)} %rhs_hbm.1, bf16[2,512,512]{2,1,0:T(8,128)(2,1)} %inverse_ref.1, bf16[2,512,256]{2,1,0:T(8,128)(2,1)} %basis_ref.1, ...), custom_call_target="tpu_custom_call" | custom-call | tf_op jit(solution)/shard_map/pallas_call | solution.py:217
  4.7 11.0 %all-to-all-start = ((bf16[4,2,256,256]{3,2,1,0:T(8,128)(2,1)}), bf16[4,2,256,256]{3,2,1,0:T(8,128)(2,1)S(1)}, u32[]{:S(2)}, u32[]{:S(2)}) async-start(bf16[4,2,256,256]{3,2,1,0:T(8,128)(2,1)} %get-tuple-element.26), calls=%async_computation | async-start | bytes 2097152 | tf_op jit(solution)/shard_map/all_to_all | solution.py:37
  15.7 2.6 %all-gather = bf16[512,256]{1,0:T(8,128)(2,1)S(1)} all-gather(bf16[256,256]{1,0:T(8,128)(2,1)S(1)} %copy-done.11), channel_id=2, replica_groups={{0,1},{2,3},{4,5},{6,7},{8,9},{10,11},{12,13},{14,15},{16,17},{18,19},{..., dimensions={0}, use_global_device_ids=true | all-gather | bytes 393216 | tf_op jit(solution)/shard_map/all_gather | solution.py:30
  18.5 5.4 %all-gather.1 = bf16[512,256]{1,0:T(8,128)(2,1)S(1)} all-gather(bf16[256,256]{1,0:T(8,128)(2,1)S(1)} %shard_map.65), channel_id=3, replica_groups={{0,2},{1,3},{4,6},{5,7},{8,10},{9,11},{12,14},{13,15},{16,18},{17,19},{..., dimensions={0}, use_global_device_ids=true | all-gather | bytes 393216 | tf_op jit(solution)/shard_map/all_gather | solution.py:30
  24.0 8.8 %all-gather.2 = bf16[512,256]{1,0:T(8,128)(2,1)S(1)} all-gather(bf16[256,256]{1,0:T(8,128)(2,1)S(1)} %shard_map.66), channel_id=4, replica_groups={{0,4},{1,5},{2,6},{3,7},{8,12},{9,13},{10,14},{11,15},{16,20},{17,21},{..., dimensions={0}, use_global_device_ids=true | all-gather | bytes 393216 | tf_op jit(solution)/shard_map/all_gather | solution.py:30
  33.0 10.1 %all-gather.3 = bf16[512,256]{1,0:T(8,128)(2,1)S(1)} all-gather(bf16[256,256]{1,0:T(8,128)(2,1)S(1)} %shard_map.67), channel_id=5, replica_groups={{0,8},{1,9},{2,10},{3,11},{4,12},{5,13},{6,14},{7,15},{16,24},{17,25},{..., dimensions={0}, use_global_device_ids=true | all-gather | bytes 393216 | tf_op jit(solution)/shard_map/all_gather | solution.py:30
  43.3 4.5 %all-gather.4 = bf16[512,256]{1,0:T(8,128)(2,1)S(1)} all-gather(bf16[256,256]{1,0:T(8,128)(2,1)S(1)} %shard_map.68), channel_id=6, replica_groups={{0,16},{32,48},{64,80},{96,112},{128,144},{160,176},{192,208},{224,240}..., dimensions={0}, use_global_device_ids=true | all-gather | bytes 393216 | tf_op jit(solution)/shard_map/all_gather | solution.py:30
  47.9 6.7 %all-gather.5 = bf16[512,256]{1,0:T(8,128)(2,1)S(1)} all-gather(bf16[256,256]{1,0:T(8,128)(2,1)S(1)} %shard_map.69), channel_id=7, replica_groups={{0,32},{16,48},{64,96},{80,112},{128,160},{144,176},{192,224},{208,240}..., dimensions={0}, use_global_device_ids=true | all-gather | bytes 393216 | tf_op jit(solution)/shard_map/all_gather | solution.py:30
  54.8 0.5 copy-done.5
  55.3 4.8 %all-gather.6 = bf16[512,256]{1,0:T(8,128)(2,1)S(1)} all-gather(bf16[256,256]{1,0:T(8,128)(2,1)S(1)} %shard_map.70), channel_id=8, replica_groups={{0,64},{16,80},{32,96},{48,112},{128,192},{144,208},{160,224},{176,240}..., dimensions={0}, use_global_device_ids=true | all-gather | bytes 393216 | tf_op jit(solution)/shard_map/all_gather | solution.py:30
  60.3 18.6 %all_to_all.10.terms_ref = bf16[4,256,256]{2,1,0:T(8,128)(2,1)S(1)} all-to-all(bf16[4,256,256]{2,1,0:T(8,128)(2,1)S(1)} %shard_map.71), channel_id=1, replica_groups={{0,128,256,384},{16,144,272,400},{32,160,288,416},{48,176,304,432},{64,..., dimensions={0} | all-to-all | bytes 1048576 | tf_op jit(solution)/shard_map/all_to_all | solution.py:37
  78.9 0.9 shard_map.72
  79.9 4.8 %all-gather.7 = bf16[512,256]{1,0:T(8,128)(2,1)S(1)} all-gather(bf16[256,256]{1,0:T(8,128)(2,1)S(1)} %get-tuple-element.29), channel_id=9, replica_groups={{0,64},{16,80},{32,96},{48,112},{128,192},{144,208},{160,224},{176,240}..., dimensions={0}, use_global_device_ids=true | all-gather | bytes 393216 | tf_op jit(solution)/shard_map/all_gather | solution.py:30
  84.7 0.4 shard_map.73
  85.1 6.0 %all-gather.8 = bf16[512,256]{1,0:T(8,128)(2,1)S(1)} all-gather(bf16[256,256]{1,0:T(8,128)(2,1)S(1)} %get-tuple-element.31), channel_id=10, replica_groups={{0,32},{16,48},{64,96},{80,112},{128,160},{144,176},{192,224},{208,240}..., dimensions={0}, use_global_device_ids=true | all-gather | bytes 393216 | tf_op jit(solution)/shard_map/all_gather | solution.py:30
  91.1 0.4 shard_map.74
  91.5 4.5 %all-gather.9 = bf16[512,256]{1,0:T(8,128)(2,1)S(1)} all-gather(bf16[256,256]{1,0:T(8,128)(2,1)S(1)} %get-tuple-element.33), channel_id=11, replica_groups={{0,16},{32,48},{64,80},{96,112},{128,144},{160,176},{192,208},{224,240}..., dimensions={0}, use_global_device_ids=true | all-gather | bytes 393216 | tf_op jit(solution)/shard_map/all_gather | solution.py:30
  96.4 8.4 %all-gather.10 = bf16[512,256]{1,0:T(8,128)(2,1)S(1)} all-gather(bf16[256,256]{1,0:T(8,128)(2,1)S(1)} %get-tuple-element.35), channel_id=12, replica_groups={{0,8},{1,9},{2,10},{3,11},{4,12},{5,13},{6,14},{7,15},{16,24},{17,25},{..., dimensions={0}, use_global_device_ids=true | all-gather | bytes 393216 | tf_op jit(solution)/shard_map/all_gather | solution.py:30
  105.3 6.8 %all-gather.11 = bf16[512,256]{1,0:T(8,128)(2,1)S(1)} all-gather(bf16[256,256]{1,0:T(8,128)(2,1)S(1)} %get-tuple-element.37), channel_id=13, replica_groups={{0,4},{1,5},{2,6},{3,7},{8,12},{9,13},{10,14},{11,15},{16,20},{17,21},{..., dimensions={0}, use_global_device_ids=true | all-gather | bytes 393216 | tf_op jit(solution)/shard_map/all_gather | solution.py:30
  112.1 0.4 shard_map.77
  112.5 8.7 %all-gather.12 = bf16[512,256]{1,0:T(8,128)(2,1)S(1)} all-gather(bf16[256,256]{1,0:T(8,128)(2,1)S(1)} %get-tuple-element.39), channel_id=14, replica_groups={{0,2},{1,3},{4,6},{5,7},{8,10},{9,11},{12,14},{13,15},{16,18},{17,19},{..., dimensions={0}, use_global_device_ids=true | all-gather | bytes 393216 | tf_op jit(solution)/shard_map/all_gather | solution.py:30
  121.2 0.4 shard_map.78
  121.7 14.6 %all-gather.13 = bf16[512,256]{1,0:T(8,128)(2,1)S(1)} all-gather(bf16[256,256]{1,0:T(8,128)(2,1)S(1)} %get-tuple-element.41), channel_id=15, replica_groups={{0,1},{2,3},{4,5},{6,7},{8,9},{10,11},{12,13},{14,15},{16,17},{18,19},{..., dimensions={0}, use_global_device_ids=true | all-gather | bytes 393216 | tf_op jit(solution)/shard_map/all_gather | solution.py:30
  136.3 2.4 %shard_map.79 = bf16[1024,256]{1,0:T(8,128)(2,1)} custom-call(s32[1,1024]{1,0:T(1,128)S(1)} %copy-done.10, bf16[2,256,256]{2,1,0:T(8,128)(2,1)S(1)} %bitcast.34, f32[256,256]{1,0:T(8,128)S(1)} %copy-done.9, bf16[256,256]{1,0:T(8,128)(2,1)S(1)} %get-tuple-element.43.above_ref, bf16[1,9,256,256]{3,2,1,0:T(8,128)(2,1)S(1)} %copy-done, ...), custom_call_target="tpu_custom_call" | custom-call | tf_op jit(solution)/shard_map/pallas_call | solution.py:257
  (33 shorter events, 2.2 us)
Async XLA Ops:
  4.7 11.0 %copy-start.11 = (bf16[256,256]{1,0:T(8,128)(2,1)S(1)}, bf16[256,256]{1,0:T(8,128)(2,1)}, u32[]{:S(2)}) copy-start(bf16[256,256]{1,0:T(8,128)(2,1)} %get-tuple-element.25) | copy-start | bytes 393220
  4.7 13.6 %copy-start = (bf16[1,9,256,256]{3,2,1,0:T(8,128)(2,1)S(1)}, bf16[1,9,256,256]{3,2,1,0:T(8,128)(2,1)}, u32[]{:S(2)}) copy-start(bf16[1,9,256,256]{3,2,1,0:T(8,128)(2,1)} %up_ref.29) | copy-start | bytes 3538948
  4.7 55.3 %all-to-all-start = ((bf16[4,2,256,256]{3,2,1,0:T(8,128)(2,1)}), bf16[4,2,256,256]{3,2,1,0:T(8,128)(2,1)S(1)}, u32[]{:S(2)}, u32[]{:S(2)}) async-start(bf16[4,2,256,256]{3,2,1,0:T(8,128)(2,1)} %get-tuple-element.26), calls=%async_computation | async-start | bytes 2097152 | tf_op jit(solution)/shard_map/all_to_all | solution.py:37
  47.8 6.9 %copy-start.3 = (bf16[512,256]{1,0:T(8,128)(2,1)}, bf16[512,256]{1,0:T(8,128)(2,1)S(1)}, u32[]{:S(2)}) copy-start(bf16[512,256]{1,0:T(8,128)(2,1)S(1)} %all-gather.4) | copy-start | bytes 786436
  54.6 0.7 copy-start.5
  60.1 18.8 %copy-start.1 = (bf16[1,9,256,256]{3,2,1,0:T(8,128)(2,1)S(1)}, bf16[1,9,256,256]{3,2,1,0:T(8,128)(2,1)}, u32[]{:S(2)}) copy-start(bf16[1,9,256,256]{3,2,1,0:T(8,128)(2,1)} %down_ref.13) | copy-start | bytes 3538948
  78.9 5.8 %copy-start.6 = (bf16[512,256]{1,0:T(8,128)(2,1)S(1)}, bf16[512,256]{1,0:T(8,128)(2,1)}, u32[]{:S(2)}) copy-start(bf16[512,256]{1,0:T(8,128)(2,1)} %copy-done.5) | copy-start | bytes 786436
  84.7 6.4 %copy-start.4 = (bf16[512,256]{1,0:T(8,128)(2,1)S(1)}, bf16[512,256]{1,0:T(8,128)(2,1)}, u32[]{:S(2)}) copy-start(bf16[512,256]{1,0:T(8,128)(2,1)} %copy-done.3) | copy-start | bytes 786436
  121.2 15.1 %copy-start.2 = (bf16[2,512,512]{2,1,0:T(8,128)(2,1)S(1)}, bf16[2,512,512]{2,1,0:T(8,128)(2,1)}, u32[]{:S(2)}) copy-start(bf16[2,512,512]{2,1,0:T(8,128)(2,1)} %inverse_ref.1) | copy-start | bytes 3145732
  121.2 15.1 %copy-start.7 = (bf16[2,512,256]{2,1,0:T(8,128)(2,1)S(1)}, bf16[2,512,256]{2,1,0:T(8,128)(2,1)}, u32[]{:S(2)}) copy-start(bf16[2,512,256]{2,1,0:T(8,128)(2,1)} %basis_ref.1) | copy-start | bytes 1572868
  121.2 15.1 %copy-start.8 = (f32[2,512,256]{2,1,0:T(8,128)S(1)}, f32[2,512,256]{2,1,0:T(8,128)}, u32[]{:S(2)}) copy-start(f32[2,512,256]{2,1,0:T(8,128)} %get-tuple-element.44.rows_ref) | copy-start | bytes 3145732
  121.2 15.1 %copy-start.9 = (f32[256,256]{1,0:T(8,128)S(1)}, f32[256,256]{1,0:T(8,128)}, u32[]{:S(2)}) copy-start(f32[256,256]{1,0:T(8,128)} %get-tuple-element.42.state_ref) | copy-start | bytes 786436
  121.2 15.1 %copy-start.10 = (s32[1,1024]{1,0:T(1,128)S(1)}, s32[1,1024]{1,0:T(1,128)}, u32[]{:S(2)}) copy-start(s32[1,1024]{1,0:T(1,128)} %order_ref.1) | copy-start | bytes 12292
